TPU v7x, 512 devices: a whole 4x8x8 slice. The times are simulated.
512 devices in a mesh: fine: 16 (over z, core), coarse: 8 (over y), comp: 4 (over x).
Axes of the slice: x: 4, y: 8, z: 8, core: 2. Of those that a mesh axis runs over, the one named last changes fastest.
Arguments:
- a_vals: bfloat16 [6144, 64, 448], P(('fine', 'coarse', 'comp')), may hold values from -0.25 to 0.25
- a_cols: int32 [6144, 7], P(('fine', 'coarse', 'comp')), may hold values from 0 to 75, as said below
- p_vals: bfloat16 [6144, 64, 256], P(('fine', 'coarse', 'comp')), may hold values from -1 to 1
- p_cols: int32 [6144, 4], P(('fine', 'coarse', 'comp')), may hold values from 0 to 7, as said below
- gp_cols: int32 [32768, 4], P(('fine', 'coarse', 'comp')), may hold values from 0 to 15, as said below
- send_list: int32 [32768], P(('fine', 'coarse', 'comp')), may hold values from 0 to 11
Outputs:
- coarse_op: float32 [16, 512, 4, 1024], P('fine', 'coarse', 'comp')
Inputs may be any that keep to these rules, and one draw needn't show every extreme that they name: `a_cols`: A value e below 12 names local row e of the same device, a value 12 + s names ghost slot s; the first entry of each row is the row itself, and every ghost slot of a device is named by at least one entry of its rows. `p_cols`: the 4 entries of a row are distinct. `gp_cols`: the 4 entries of a row are distinct.
All inputs are finite; a program needn't handle non-finite values.
Results may differ from a plain program's by a relative error of at most 0.0029.
Values may be sent and summed in bfloat16 or wider, within the bound.
No kernel may reach another device: no remote copies, remote signals or barrier semaphores. Data moves between devices by JAX's collectives and lax.ppermute only.
A program may use at most 64 MiB of HBM per device.

v0:
```python
import jax
import jax.numpy as jnp
from jax import lax
from jax.sharding import PartitionSpec as P

NC = 8
EXT = 8


def local_terms(a_rows, a_index, p_rows, p_index, ghosts, g_index):
    block_rows = a_rows.shape[0]
    block_size = a_rows.shape[1]
    pick_count = p_index.shape[1]
    link_count = a_index.shape[1]
    columns_all = NC + EXT
    sources = jnp.concatenate([p_rows, ghosts], axis=0)
    source_cols = jnp.concatenate([p_index, g_index], axis=0)
    fetched = jnp.take(sources, a_index, axis=0)
    fetched_cols = jnp.take(source_cols, a_index, axis=0)
    column_ids = jnp.arange(columns_all, dtype=jnp.int32)
    placing = (fetched_cols[:, :, :, None] == column_ids[None, None, None, :]).astype(jnp.float32)
    a_split = a_rows.reshape(block_rows, block_size, link_count, block_size)
    terms = jnp.einsum("riam,ramn->rain", a_split, fetched, preferred_element_type=jnp.float32)
    terms = terms.reshape(block_rows, block_size, link_count, pick_count, block_size)
    applied = jnp.einsum("rakc,riakj->ricj", placing, terms, precision=lax.Precision.HIGHEST)
    prod_rows = applied.astype(jnp.bfloat16).reshape(
        block_rows * block_size, columns_all * block_size
    )
    own_rows = p_rows.reshape(block_rows, block_size, pick_count, block_size)
    owned_ids = jnp.arange(NC, dtype=jnp.int32)
    spread = jnp.zeros((block_rows, block_size, NC, block_size), jnp.bfloat16)
    for pick in range(pick_count):
        hits = p_index[:, pick, None] == owned_ids[None, :]
        spread = jnp.where(hits[:, None, :, None], own_rows[:, :, pick, None, :], spread)
    spread = spread.reshape(block_rows * block_size, NC * block_size)
    return (spread, prod_rows)


def contract(spread, prod_rows):
    return lax.dot_general(
        spread, prod_rows, (((0,), (0,)), ((), ())), preferred_element_type=jnp.float32
    )


def on_device(a_vals, a_cols, p_vals, p_cols, gp_cols, send_list):
    outgoing = jnp.take(p_vals, send_list, axis=0)
    arrived = lax.all_to_all(outgoing, ("fine", "comp"), split_axis=0, concat_axis=0, tiled=True)
    spread, prod_rows = local_terms(a_vals, a_cols, p_vals, p_cols, arrived, gp_cols)
    owned = lax.psum_scatter(contract(spread, prod_rows), "coarse", scatter_dimension=0, tiled=True)
    return owned.reshape((1, owned.shape[0], 1, owned.shape[1]))


def solution(mesh):
    placed = (
        P(("fine", "coarse", "comp"), None, None),
        P(("fine", "coarse", "comp"), None),
        P(("fine", "coarse", "comp"), None, None),
        P(("fine", "coarse", "comp"), None),
        P(("fine", "coarse", "comp"), None),
        P(("fine", "coarse", "comp")),
    )
    return jax.shard_map(
        on_device,
        mesh=mesh,
        in_specs=placed,
        out_specs=P("fine", "coarse", "comp", None),
        check_vma=False,
    )
```

profile of v0, /device:TPU:6, one launch (start us, length us, event | category | flops | bytes accessed | tf_op | source)
XLA Modules:
  0.0 163.5 jit_solution(15291214799395022681)
XLA Ops:
  6.5 0.7 compare_select_fusion.1
  7.2 0.7 compare_and_fusion.1
  7.9 1.7 %gather_fusion = bf16[64,64,256]{2,1,0:T(8,128)(2,1)S(1)} fusion(bf16[12,64,256]{2,1,0:T(8,128)(2,1)} %param.8, s32[1024]{0:T(1024)S(1)} %pad_clamp_fusion.1), kind=kCustom, calls=%fused_computation | custom fusion | bytes 4194560 | tf_op jit(solution)/shard_map/jit(_take)/gather | solution.py:46
  9.5 1.6 broadcast_select_fusion
  11.1 14.1 %all-to-all-start = ((bf16[64,64,256]{2,1,0:T(8,128)(2,1)}), bf16[64,64,256]{2,1,0:T(8,128)(2,1)}, u32[]{:S(2)}, u32[]{:S(2)}) async-start(bf16[64,64,256]{2,1,0:T(8,128)(2,1)} %broadcast_select_fusion), calls=%async_computation | async-start | bytes 4194304 | tf_op jit(solution)/shard_map/all_to_all | solution.py:47
  25.3 0.3 reshape.149
  25.8 1.7 %fusion.13 = (bf16[12,64,1,64]{3,2,1,0:T(2,128)(2,1)S(1)}, bf16[12,64,1,64]{3,2,1,0:T(2,128)(2,1)S(1)}, bf16[12,64,1,64]{3,2,1,0:T(2,128)(2,1)S(1)}, bf16[12,64,1,64]{3,2,1,0:T(2,128)(2,1)S(1)}) fusion(bf16[12,64,4,64]{3,2,1,0:T(4,128)(2,1)S(1)} %reshape.149), kind=kLoop, calls=%fused_computation.38 | loop fusion | bytes 786432 | tf_op jit(solution)/shard_map/slice | solution.py:34
  27.7 0.9 select_select_fusion
  28.6 1.7 %select_n.79 = bf16[768,512]{1,0:T(8,128)(2,1)} reshape(bf16[12,64,8,64]{3,2,1,0:T(8,128)(2,1)S(1)} %select_select_fusion) | data formatting | bytes 1572864 | tf_op jit(solution)/shard_map/jit(_where)/select_n | solution.py:34
  30.5 0.1 copy.35
  30.6 1.9 %reshape.150 = bf16[12,64,7,64]{3,2,1,0:T(8,128)(2,1)} reshape(bf16[12,64,448]{2,1,0:T(8,128)(2,1)S(1)} %copy-done.1) | data formatting | bytes 1376256 | tf_op jit(solution)/shard_map/reshape | solution.py:22
  32.6 0.1 copy.39
  32.7 0.6 gather_fusion.2
  33.5 0.8 copy.41
  34.3 42.2 %all-to-all-done = bf16[64,64,256]{2,1,0:T(8,128)(2,1)} async-done(((bf16[64,64,256]{2,1,0:T(8,128)(2,1)}), bf16[64,64,256]{2,1,0:T(8,128)(2,1)}, u32[]{:S(2)}, u32[]{:S(2)}) %all-to-all-start) | async-done | bytes 2097184 | tf_op jit(solution)/shard_map/all_to_all | solution.py:47
  76.5 1.8 %pad_maximum_fusion = bf16[76,64,256]{2,1,0:T(8,128)(2,1)S(1)} fusion(bf16[64,64,256]{2,1,0:T(8,128)(2,1)} %all-to-all-done, bf16[12,64,256]{2,1,0:T(8,128)(2,1)S(1)} %copy-done), kind=kLoop, calls=%fused_computation.8 | loop fusion | flops 1245184 | bytes 4980736 | tf_op jit(solution)/shard_map/concatenate | solution.py:16
  78.3 2.4 %gather_fusion.1 = bf16[84,64,256]{2,1,0:T(8,128)(2,1)} fusion(bf16[76,64,256]{2,1,0:T(8,128)(2,1)S(1)} %pad_maximum_fusion, s32[1024]{0:T(1024)S(1)} %pad_clamp_fusion), kind=kCustom, calls=%fused_computation.1 | custom fusion | bytes 5505360 | tf_op jit(solution)/shard_map/jit(_take)/gather | solution.py:18
  80.7 5.6 %fusion.4 = f32[12,7,64,256]{3,2,1,0:T(8,128)} fusion(bf16[12,7,64,256]{3,2,1,0:T(8,128)(2,1)} %bitcast.43, pred[12,7]{1,0:T(8,128)(4,1)S(1)} %copy.35, bf16[12,64,7,64]{3,2,1,0:T(8,128)(2,1)} %reshape.150), kind=kOutput, calls=%fused_computation.9 | convolution fusion | flops 177537024 | bytes 8945748 | tf_op jit(solution)/shard_map/riam,ramn->rain/dot_general | solution.py:23
  86.3 10.1 %reshape.151 = f32[12,64,7,4,64]{4,3,2,1,0:T(4,128)} reshape(f32[12,7,64,256]{3,2,1,0:T(8,128)} %fusion.4) | data formatting | bytes 11010048 | tf_op jit(solution)/shard_map/reshape | solution.py:24
  96.4 10.6 %fusion = bf16[12,64,16,64]{3,2,1,0:T(8,128)(2,1)S(1)} fusion(f32[12,64,7,4,64]{4,3,2,1,0:T(4,128)} %reshape.151, s32[12,7,4]{2,1,0:T(8,128)S(1)} %copy-done.2), kind=kOutput, calls=%fused_computation.4 | convolution fusion | flops 265032960 | bytes 7079232 | tf_op jit(solution)/shard_map/rakc,riakj->ricj/dot_general | solution.py:25
  107.0 3.2 %reshape.152 = bf16[768,1024]{1,0:T(8,128)(2,1)} reshape(bf16[12,64,16,64]{3,2,1,0:T(8,128)(2,1)S(1)} %fusion) | data formatting | bytes 3145728 | tf_op jit(solution)/shard_map/reshape | solution.py:26
  110.2 4.0 %fusion.14 = f32[512,1024]{1,0:T(8,128)} fusion(bf16[768,512]{1,0:T(8,128)(2,1)} %select_n.79, bf16[768,1024]{1,0:T(8,128)(2,1)} %reshape.152), kind=kOutput, calls=%fused_computation.39 | convolution fusion | flops 805306368 | bytes 4456448 | tf_op jit(solution)/shard_map/dot_general | solution.py:40
  114.2 40.6 %reduce-scatter.2.cloned.1.call-done = f32[64,1024]{1,0:T(8,128)} async-done(((f32[512,1024]{1,0:T(8,128)}), f32[64,1024]{1,0:T(8,128)}) %reduce-scatter.2.cloned.1.call-update) | async-done | bytes 262160 | tf_op jit(solution)/shard_map/reduce_scatter | solution.py:49
  154.8 1.9 %copy.42 = f32[1,64,1,1024]{3,2,1,0:T(1,128)} copy(f32[1,64,1,1024]{3,1,2,0:T(8,128)} %bitcast.44) | data formatting | bytes 524288 | tf_op jit(solution)/shard_map/reshape | solution.py:50
  (29 shorter events, 0.8 us)
Async XLA Ops:
  11.1 14.2 %copy-start = (bf16[12,64,256]{2,1,0:T(8,128)(2,1)S(1)}, bf16[12,64,256]{2,1,0:T(8,128)(2,1)}, u32[]{:S(2)}) copy-start(bf16[12,64,256]{2,1,0:T(8,128)(2,1)} %param.8) | copy-start | bytes 1179652
  11.1 14.5 %copy-start.4 = (s32[12,4]{0,1:T(4,128)S(1)}, s32[12,4]{0,1:T(4,128)}, u32[]{:S(2)}) copy-start(s32[12,4]{0,1:T(4,128)} %param.9) | copy-start | bytes 580
  11.1 65.3 %all-to-all-start = ((bf16[64,64,256]{2,1,0:T(8,128)(2,1)}), bf16[64,64,256]{2,1,0:T(8,128)(2,1)}, u32[]{:S(2)}, u32[]{:S(2)}) async-start(bf16[64,64,256]{2,1,0:T(8,128)(2,1)} %broadcast_select_fusion), calls=%async_computation | async-start | bytes 4194304 | tf_op jit(solution)/shard_map/all_to_all | solution.py:47
  25.3 129.5 %reduce-scatter.2.cloned.1.call-start = ((), (), s32[]{:S(2)}) async-start(), calls=%async_computation.2 | async-start | bytes 2359296 | tf_op jit(solution)/shard_map/reduce_scatter | solution.py:49
  27.6 2.7 %copy-start.3 = (s32[12,7]{0,1:T(8,128)S(1)}, s32[12,7]{0,1:T(8,128)}, u32[]{:S(2)}) copy-start(s32[12,7]{0,1:T(8,128)} %param.7) | copy-start | bytes 1012
  27.7 3.0 %copy-start.1 = (bf16[12,64,448]{2,1,0:T(8,128)(2,1)S(1)}, bf16[12,64,448]{2,1,0:T(8,128)(2,1)}, u32[]{:S(2)}) copy-start(bf16[12,64,448]{2,1,0:T(8,128)(2,1)} %param.6) | copy-start | bytes 2064388
  28.6 3.9 %copy-start.5 = (s32[64,4]{0,1:T(4,128)S(1)}, s32[64,4]{0,1:T(4,128)}, u32[]{:S(2)}) copy-start(s32[64,4]{0,1:T(4,128)} %param.10) | copy-start | bytes 3076
  86.3 10.1 %copy-start.2 = (s32[12,7,4]{2,1,0:T(8,128)S(1)}, s32[12,7,4]{2,1,0:T(8,128)}, u32[]{:S(2)}) copy-start(s32[12,7,4]{2,1,0:T(8,128)} %copy.41) | copy-start | bytes 4036
Sparse Core Ops, SparseCore 0:
  114.3 40.4 reduce-scatter.1
where the time goes:
time: 164 us
  waiting for transfers between devices  82.7 us (50%)
  local copies, waits for them, and re-layouts  27 us (16%)
  matrix products  20.1 us (12%)
  starting transfers between devices  14.2 us (9%)
  between operations  13.5 us (8%)
  other arithmetic  5.9 us (4%)
    all_to_all x1, waiting for transfers between devices, on_device(): lax.all_to_all(outgoing, ('fine', 'comp'), split_axis=0, concat_axis=0, t...  42.2 us
    reduce_scatter x1, waiting for transfers between devices, on_device(): lax.psum_scatter(contract(spread, prod_rows), 'coarse', scatter_dimension...  40.6 us
    all_to_all x1, starting transfers between devices, on_device(): lax.all_to_all(outgoing, ('fine', 'comp'), split_axis=0, concat_axis=0, t...  14.1 us
    dot_general x1, matrix products, local_terms(): jnp.einsum('rakc,riakj->ricj', placing, terms, precision=lax.Precision.HI...  10.6 us
    reshape x1, local copies, waits for them, and re-layouts, local_terms(): terms.reshape(block_rows, block_size, link_count, pick_count, block_size)  10.1 us
    dot_general x1, matrix products, local_terms(): jnp.einsum('riam,ramn->rain', a_split, fetched, preferred_element_type=jn...  5.55 us
    dot_general x1, matrix products, contract(): lax.dot_general(spread, prod_rows, (((0,), (0,)), ((), ())), preferred_el...  3.99 us
  transfers between devices with their start and end apart: 2, of which 2 were waited for; matrix products, arithmetic and copies ran while one was open for 5% of the time, Pallas kernels for 0%

commit v1 on v0

v1 whole, which is shorter than its diff:
```python
import jax
import jax.numpy as jnp
from jax import lax
from jax.experimental import pallas as pl
from jax.experimental.pallas import tpu as pltpu
from jax.sharding import PartitionSpec as P

NC = 8
EXT = 8
WIDTHS = (32, 32)

NT = (((1,), (1,)), ((), ()))
NN = (((1,), (0,)), ((), ()))
VMEM_LIMIT = 48 * 1024 * 1024


def starts_of(widths):
    return [sum(widths[:c]) for c in range(len(widths))]


def pack_kernel(widths, send_ref, p_ref, *outs):
    rows, size, _ = p_ref.shape
    count = len(widths)
    local, sent = outs[:count], outs[count:]
    flat = p_ref[...].reshape(rows * size, 4 * size)
    row = lax.broadcasted_iota(jnp.int32, (2 * size, 4 * size), 0)
    col = lax.broadcasted_iota(jnp.int32, (2 * size, 4 * size), 1)
    wanted = jnp.zeros_like(row)
    base = 0
    for w, start in zip(widths, starts_of(widths)):
        for h in range(2):
            inside = (row >= base) & (row < base + w)
            wanted = jnp.where(inside, 2 * h * size + start + row - base, wanted)
            base += w
    turned = []
    for l in range(2):
        pick = (col == wanted + l * size).astype(jnp.float32).astype(jnp.bfloat16)
        turned.append(lax.dot_general(pick, flat, NT, preferred_element_type=jnp.float32))
    lane = lax.broadcasted_iota(jnp.int32, (2 * size, 2 * size), 1)
    for u in range(rows // 2):
        low = turned[0][:, u * 2 * size : (u + 1) * 2 * size]
        high = turned[1][:, u * 2 * size : (u + 1) * 2 * size]
        first = jnp.where(lane < size, low, pltpu.roll(high, size, 1)).astype(jnp.bfloat16)
        second = jnp.where(lane < size, pltpu.roll(low, size, 1), high).astype(jnp.bfloat16)
        base = 0
        for c, w in enumerate(widths):
            local[c][2 * u] = first[base : base + 2 * w]
            local[c][2 * u + 1] = second[base : base + 2 * w]
            base += 2 * w
    for c in range(count):
        for s in range(sent[c].shape[0]):
            sent[c][s] = local[c][send_ref[s]]


def pack(widths, send_list, p_vals):
    rows, size, _ = p_vals.shape
    slots = send_list.shape[0]
    vmem = pl.BlockSpec(memory_space=pltpu.VMEM)
    shapes = [jax.ShapeDtypeStruct((rows, 2 * w, 2 * size), p_vals.dtype) for w in widths]
    shapes += [jax.ShapeDtypeStruct((slots, 2 * w, 2 * size), p_vals.dtype) for w in widths]
    outs = pl.pallas_call(
        lambda *refs: pack_kernel(widths, *refs),
        out_shape=shapes,
        in_specs=[pl.BlockSpec(memory_space=pltpu.SMEM), vmem],
        out_specs=[vmem] * len(shapes),
        compiler_params=pltpu.CompilerParams(vmem_limit_bytes=VMEM_LIMIT),
        name="pack",
    )(send_list, p_vals)
    return outs[: len(widths)], outs[len(widths) :]


def prepare_kernel(p_cols_ref, p_ref, a_ref, spread_ref, mixed_ref, stacked):
    rows, size, _ = p_ref.shape
    width = a_ref.shape[2]
    links = width // size
    flat = p_ref[...].reshape(rows * size, 4 * size)
    row = lax.broadcasted_iota(jnp.int32, (4 * size, 4 * size), 0)
    col = lax.broadcasted_iota(jnp.int32, (4 * size, 4 * size), 1)
    eye = (row == col).astype(jnp.float32).astype(jnp.bfloat16)
    turned = lax.dot_general(eye, flat, NT, preferred_element_type=jnp.float32).astype(jnp.bfloat16)
    spread_ref[...] = jnp.zeros_like(spread_ref)
    for r in range(rows):
        for k in range(4):
            start = pl.multiple_of(p_cols_ref[k, r] * size, size)
            spread_ref[pl.ds(start, size), r * size : (r + 1) * size] = turned[
                k * size : (k + 1) * size, r * size : (r + 1) * size
            ]
    for r in range(rows):
        for a in range(links):
            stacked[a * size : (a + 1) * size, r * size : (r + 1) * size] = a_ref[r, :, a * size : (a + 1) * size]
    row = lax.broadcasted_iota(jnp.int32, (width, width), 0)
    col = lax.broadcasted_iota(jnp.int32, (width, width), 1)
    pair = links * (row % size) + row // size
    pick = (col == pair).astype(jnp.float32).astype(jnp.bfloat16)
    keep = (col // size == pair // size).astype(jnp.float32).astype(jnp.bfloat16)
    moved = lax.dot_general(pick, stacked[...], NN, preferred_element_type=jnp.float32).astype(jnp.bfloat16)
    for r in range(rows):
        part = moved[:, r * size : (r + 1) * size]
        mixed_ref[r] = jnp.concatenate([part] * links, axis=1) * keep


def prepare(p_cols, p_vals, a_vals):
    rows, size, _ = p_vals.shape
    width = a_vals.shape[2]
    vmem = pl.BlockSpec(memory_space=pltpu.VMEM)
    return pl.pallas_call(
        prepare_kernel,
        out_shape=[
            jax.ShapeDtypeStruct((NC * size, rows * size), p_vals.dtype),
            jax.ShapeDtypeStruct((rows, width, width), p_vals.dtype),
        ],
        in_specs=[pl.BlockSpec(memory_space=pltpu.SMEM), vmem, vmem],
        out_specs=[vmem, vmem],
        scratch_shapes=[pltpu.VMEM((width, rows * size), jnp.bfloat16)],
        compiler_params=pltpu.CompilerParams(vmem_limit_bytes=VMEM_LIMIT),
        name="prepare",
    )(p_cols.T, p_vals, a_vals)


def product_kernel(a_cols_ref, p_cols_ref, g_cols_ref, mixed_ref, spread_ref, local_ref, ghost_ref, out_ref, sources, cols, picked, terms, prod, sems, *sums):
    rows, width, _ = mixed_ref.shape
    links = a_cols_ref.shape[0]
    size = width // links
    w = local_ref.shape[1] // 2
    slots = ghost_ref.shape[0]
    copies = [
        pltpu.make_async_copy(local_ref, sources.at[pl.ds(0, rows)], sems.at[0]),
        pltpu.make_async_copy(ghost_ref, sources.at[pl.ds(rows, slots)], sems.at[1]),
    ]
    for copy in copies:
        copy.start()
    for r in range(rows):
        sums[r][...] = jnp.zeros_like(sums[r])
    for k in range(4):
        for e in range(rows):
            cols[k, e] = p_cols_ref[k, e]
        for e in range(slots):
            cols[k, rows + e] = g_cols_ref[k, e]
    for copy in copies:
        copy.wait()
    for r in range(rows):
        for a in range(links):
            e = a_cols_ref[a, r]
            for k in range(4):
                h, l = divmod(k, 2)
                picked[r, k * w : (k + 1) * w, a * size : (a + 1) * size] = sources[
                    e, h * w : (h + 1) * w, l * size : (l + 1) * size
                ]
        terms[r] = lax.dot_general(picked[r], mixed_ref[r], NT, preferred_element_type=jnp.float32)
    for a in range(links):
        for k in range(4):
            for r in range(rows):
                start = pl.multiple_of(cols[k, a_cols_ref[a, r]] * w, w)
                here = pl.ds(start, w)
                sums[r][here, :] = sums[r][here, :] + terms[r, k * w : (k + 1) * w, a * size : (a + 1) * size]
    for r in range(rows):
        prod[:, r * size : (r + 1) * size] = sums[r][...].astype(jnp.bfloat16)
    out_ref[...] = lax.dot_general(
        spread_ref[...], prod[...], NT, preferred_element_type=jnp.float32
    ).astype(jnp.bfloat16)


def product(a_cols, p_cols, gp_cols, mixed, spread_rows, local, ghosts):
    rows, width, _ = mixed.shape
    slots, double, lanes = ghosts.shape
    size = lanes // 2
    wide = (NC + EXT) * (double // 2)
    vmem = pl.BlockSpec(memory_space=pltpu.VMEM)
    smem = pl.BlockSpec(memory_space=pltpu.SMEM)
    anywhere = pl.BlockSpec(memory_space=pl.ANY)
    return pl.pallas_call(
        product_kernel,
        out_shape=jax.ShapeDtypeStruct((NC * size, wide), jnp.bfloat16),
        in_specs=[smem, smem, smem, vmem, vmem, anywhere, anywhere],
        out_specs=vmem,
        scratch_shapes=[
            pltpu.VMEM((rows + slots, double, lanes), jnp.bfloat16),
            pltpu.SMEM((4, rows + slots), jnp.int32),
            pltpu.VMEM((rows, 2 * double, width), jnp.bfloat16),
            pltpu.VMEM((rows, 2 * double, width), jnp.float32),
            pltpu.VMEM((wide, rows * size), jnp.bfloat16),
            pltpu.SemaphoreType.DMA((2,)),
        ]
        + [pltpu.VMEM((wide, size), jnp.float32)] * rows,
        compiler_params=pltpu.CompilerParams(vmem_limit_bytes=VMEM_LIMIT),
        name="product",
    )(a_cols.T, p_cols.T, gp_cols.T, mixed, spread_rows, local, ghosts)


def total_kernel(widths, *refs):
    parts, out_ref = refs[:-1], refs[-1]
    size = out_ref.shape[0]
    for part, w, start in zip(parts, widths, starts_of(widths)):
        total = part[0].astype(jnp.float32)
        for c in range(1, part.shape[0]):
            total = total + part[c].astype(jnp.float32)
        for j in range(NC + EXT):
            out_ref[:, 0, j * size + start : j * size + start + w] = total[:, j * w : (j + 1) * w]


def total(widths, parts):
    size = parts[0].shape[1]
    vmem = pl.BlockSpec(memory_space=pltpu.VMEM)
    return pl.pallas_call(
        lambda *refs: total_kernel(widths, *refs),
        out_shape=jax.ShapeDtypeStruct((size, 1, (NC + EXT) * size), jnp.float32),
        in_specs=[vmem] * len(parts),
        out_specs=vmem,
        compiler_params=pltpu.CompilerParams(vmem_limit_bytes=VMEM_LIMIT),
        name="total",
    )(*parts)


def on_device(a_vals, a_cols, p_vals, p_cols, gp_cols, send_list):
    size = p_vals.shape[1]
    local, outgoing = pack(WIDTHS, send_list, p_vals)
    spread_rows, mixed = prepare(p_cols, p_vals, a_vals)
    parts = []
    for c in range(len(WIDTHS)):
        arrived = lax.all_to_all(outgoing[c], ("fine", "comp"), split_axis=0, concat_axis=0, tiled=True)
        partial = product(a_cols, p_cols, gp_cols, mixed, spread_rows, local[c], arrived)
        moved = lax.all_to_all(partial, "coarse", split_axis=0, concat_axis=0, tiled=True)
        parts.append(moved.reshape(NC, size, -1))
    owned = total(WIDTHS, parts)
    return owned.reshape((1, owned.shape[0], 1, owned.shape[2]))


def solution(mesh):
    placed = (
        P(("fine", "coarse", "comp"), None, None),
        P(("fine", "coarse", "comp"), None),
        P(("fine", "coarse", "comp"), None, None),
        P(("fine", "coarse", "comp"), None),
        P(("fine", "coarse", "comp"), None),
        P(("fine", "coarse", "comp")),
    )
    return jax.shard_map(
        on_device,
        mesh=mesh,
        in_specs=placed,
        out_specs=P("fine", "coarse", "comp", None),
        check_vma=False,
    )
```

time: 164 us -> 127 us (0.77); the launches traced: 164 us -> 125 us
  blocking collectives: 0 us -> 60.6 us
  waiting for transfers between devices: 82.7 us -> 25.4 us
  local copies, waits for them, and re-layouts: 27 us -> 4.47 us
  Pallas kernels: 0 us -> 21.6 us
  matrix products: 20.1 us -> 0 us
  between operations: 13.5 us -> 0.05 us
  other arithmetic: 5.9 us -> 0 us
  starting transfers between devices: 14.2 us -> 12.5 us
    all_to_all x0 -> x2, blocking collectives: none -> 60.6 us  [the longest x1 42.4 us: on_device(): lax.all_to_all(outgoing[c], ('fine', 'comp'), split_axis=0, concat_axis=0...]
    reduce_scatter x1 -> x0, waiting for transfers between devices: 40.6 us -> none  [on_device(): lax.psum_scatter(contract(spread, prod_rows), 'coarse', scatter_dimension...]
    pallas_call x0 -> x5, Pallas kernels: none -> 21.6 us  [the longest x2 12.6 us: product(): pl.pallas_call(product_kernel, out_shape=jax.ShapeDtypeStruct((NC * size,...]
    dot_general x3 -> x0, matrix products: 20.1 us -> none  [the longest x1 10.6 us: local_terms(): jnp.einsum('rakc,riakj->ricj', placing, terms, precision=lax.Precision.HI...]
    reshape x5 -> x0, local copies, waits for them, and re-layouts: 17.4 us -> none  [the longest x1 10.1 us: local_terms(): terms.reshape(block_rows, block_size, link_count, pick_count, block_size)]
    all_to_all x1 -> x2, waiting for transfers between devices: 42.2 us -> 25.4 us  [the longest x1 14.8 us: on_device(): lax.all_to_all(outgoing[c], ('fine', 'comp'), split_axis=0, concat_axis=0...]
    gather x5 -> x0, local copies, waits for them, and re-layouts: 4.88 us -> none  [the longest x1 2.44 us: local_terms(): fetched = jnp.take(sources, a_index, axis=0)]
    unnamed x14 -> x16, local copies, waits for them, and re-layouts: 0.16 us -> 4.47 us
  transfers between devices with their start and end apart: 2 -> 2, of which waited for: 2 -> 2; matrix products, arithmetic and copies ran while one was open for 5% -> 0% of each run, Pallas kernels for 0% -> 14%
where the time goes in v1:
time: 127 us; the launch traced here: 125 us
  blocking collectives  60.6 us (48%)
  waiting for transfers between devices  25.4 us (20%)
  Pallas kernels  21.6 us (17%)
  starting transfers between devices  12.5 us (10%)
  local copies, waits for them, and re-layouts  4.47 us (4%)
    all_to_all x1, blocking collectives, on_device(): lax.all_to_all(outgoing[c], ('fine', 'comp'), split_axis=0, concat_axis=0...  42.4 us
    all_to_all x1, blocking collectives, on_device(): lax.all_to_all(partial, 'coarse', split_axis=0, concat_axis=0, tiled=True)  18.2 us
    all_to_all x1, waiting for transfers between devices, on_device(): lax.all_to_all(outgoing[c], ('fine', 'comp'), split_axis=0, concat_axis=0...  14.8 us
    pallas_call x2, Pallas kernels, product(): pl.pallas_call(product_kernel, out_shape=jax.ShapeDtypeStruct((NC * size,...  12.6 us
    all_to_all x1, waiting for transfers between devices, on_device(): lax.all_to_all(partial, 'coarse', split_axis=0, concat_axis=0, tiled=True)  10.6 us
    all_to_all x1, starting transfers between devices, on_device(): lax.all_to_all(partial, 'coarse', split_axis=0, concat_axis=0, tiled=True)  7.11 us
    all_to_all x1, starting transfers between devices, on_device(): lax.all_to_all(outgoing[c], ('fine', 'comp'), split_axis=0, concat_axis=0...  5.41 us
    pallas_call x1, Pallas kernels, prepare(): pl.pallas_call(prepare_kernel, out_shape=[jax.ShapeDtypeStruct((NC * size...  4.52 us
  transfers between devices with their start and end apart: 2, of which 2 were waited for; matrix products, arithmetic and copies ran while one was open for 0% of the time, Pallas kernels for 14%

profile of v1, /device:TPU:6, one launch (start us, length us, event | category | flops | bytes accessed | tf_op | source)
XLA Modules:
  0.0 124.7 jit_solution(6345506465038118909)
XLA Ops:
  0.0 0.0 copy-start
  0.0 1.0 copy-done
  1.0 0.0 copy-start.7
  1.0 0.7 copy-done.7
  1.7 0.0 copy-start.5
  1.7 0.0 copy-start.6
  1.7 2.1 %pack.1 = (bf16[12,64,128]{2,1,0:T(8,128)(2,1)S(1)}, bf16[12,64,128]{2,1,0:T(8,128)(2,1)S(1)}, bf16[64,64,128]{2,1,0:T(8,128)(2,1)}, bf16[64,64,128]{2,1,0:T(8,128)(2,1)S(1)}) custom-call(s32[64]{0:T(128)S(1)} %copy-done.7, bf16[12,64,256]{2,1,0:T(8,128)(2,1)S(1)} %copy-done), custom_call_target="tpu_custom_call" | custom-call | tf_op jit(solution)/shard_map/pack/pallas_call | solution.py:61
  3.8 42.4 %all_to_all.28.ghost_ref = bf16[64,64,128]{2,1,0:T(8,128)(2,1)S(1)} all-to-all(bf16[64,64,128]{2,1,0:T(8,128)(2,1)S(1)} %get-tuple-element.16), channel_id=1, replica_groups=mesh['fine'=16,'coarse'=8,'comp'=4] {'fine','comp'}, dimensions={0} | all-to-all | bytes 2097152 | tf_op jit(solution)/shard_map/all_to_all | solution.py:220
  46.2 5.4 %all-to-all-start = ((bf16[64,64,128]{2,1,0:T(8,128)(2,1)}), bf16[64,64,128]{2,1,0:T(8,128)(2,1)S(1)}, u32[]{:S(2)}, u32[]{:S(2)}) async-start(bf16[64,64,128]{2,1,0:T(8,128)(2,1)} %get-tuple-element.14), calls=%async_computation | async-start | bytes 2097152 | tf_op jit(solution)/shard_map/all_to_all | solution.py:220
  51.6 0.0 copy-start.1
  51.6 1.0 copy-done.1
  52.6 1.1 copy-done.2
  53.7 0.7 copy-done.3
  54.4 4.5 %prepare.1 = (bf16[512,768]{1,0:T(8,128)(2,1)S(1)}, bf16[12,448,448]{2,1,0:T(8,128)(2,1)}) custom-call(s32[4,12]{1,0:T(4,128)S(1)} %bitcast.7, bf16[12,64,256]{2,1,0:T(8,128)(2,1)S(1)} %copy-done.1, bf16[12,64,448]{2,1,0:T(8,128)(2,1)S(1)} %copy-done.2), custom_call_target="tpu_custom_call" | custom-call | tf_op jit(solution)/shard_map/prepare/pallas_call | solution.py:106
  58.9 0.0 copy-done.5
  58.9 0.0 copy-done.6
  58.9 6.7 %product.3 = bf16[512,512]{1,0:T(8,128)(2,1)} custom-call(s32[7,12]{1,0:T(8,128)S(1)} %bitcast.10, s32[4,12]{1,0:T(4,128)S(1)} %bitcast.8, s32[4,64]{1,0:T(4,128)S(1)} %bitcast.12, bf16[12,448,448]{2,1,0:T(8,128)(2,1)} %get-tuple-element.11.mixed_ref, bf16[512,768]{1,0:T(8,128)(2,1)S(1)} %get-tuple-element.12.spread_ref, ...), custom_call_target="tpu_custom_call" | custom-call | tf_op jit(solution)/shard_map/product/pallas_call | solution.py:171
  65.6 14.8 %all-to-all-done.ghost_ref = bf16[64,64,128]{2,1,0:T(8,128)(2,1)S(1)} async-done(((bf16[64,64,128]{2,1,0:T(8,128)(2,1)}), bf16[64,64,128]{2,1,0:T(8,128)(2,1)S(1)}, u32[]{:S(2)}, u32[]{:S(2)}) %all-to-all-start) | async-done | bytes 1048608 | tf_op jit(solution)/shard_map/all_to_all | solution.py:220
  80.4 7.1 %all-to-all-start.3 = ((bf16[8,64,512]{2,1,0:T(8,128)(2,1)}), bf16[8,64,512]{2,1,0:T(8,128)(2,1)S(1)}, u32[]{:S(2)}, u32[]{:S(2)}) async-start(bf16[8,64,512]{2,1,0:T(8,128)(2,1)} %bitcast.4), calls=%async_computation.3 | async-start | bytes 1048576 | tf_op jit(solution)/shard_map/all_to_all | solution.py:222
  87.5 0.0 copy-done.4
  87.5 5.9 %product.2 = bf16[512,512]{1,0:T(8,128)(2,1)S(1)} custom-call(s32[7,12]{1,0:T(8,128)S(1)} %bitcast.11, s32[4,12]{1,0:T(4,128)S(1)} %bitcast.9, s32[4,64]{1,0:T(4,128)S(1)} %bitcast.13, bf16[12,448,448]{2,1,0:T(8,128)(2,1)} %get-tuple-element.11.mixed_ref, bf16[512,768]{1,0:T(8,128)(2,1)S(1)} %get-tuple-element.12.spread_ref, ...), custom_call_target="tpu_custom_call" | custom-call | tf_op jit(solution)/shard_map/product/pallas_call | solution.py:171
  93.4 10.6 %all-to-all-done.3.refs_1_ = bf16[8,64,512]{2,1,0:T(8,128)(2,1)S(1)} async-done(((bf16[8,64,512]{2,1,0:T(8,128)(2,1)}), bf16[8,64,512]{2,1,0:T(8,128)(2,1)S(1)}, u32[]{:S(2)}, u32[]{:S(2)}) %all-to-all-start.3) | async-done | bytes 524320 | tf_op jit(solution)/shard_map/all_to_all | solution.py:222
  104.0 18.2 %all_to_all.29.refs_0_ = bf16[8,64,512]{2,1,0:T(8,128)(2,1)S(1)} all-to-all(bf16[8,64,512]{2,1,0:T(8,128)(2,1)S(1)} %bitcast.6), channel_id=1, replica_groups=mesh['fine'=16,'coarse'=8,'comp'=4] {'coarse'}, dimensions={0} | all-to-all | bytes 1048576 | tf_op jit(solution)/shard_map/all_to_all | solution.py:222
  122.3 2.4 %total.1 = f32[64,1,1024]{2,1,0:T(1,128)} custom-call(bf16[8,64,512]{2,1,0:T(8,128)(2,1)S(1)} %all_to_all.29.refs_0_, bf16[8,64,512]{2,1,0:T(8,128)(2,1)S(1)} %all-to-all-done.3.refs_1_), custom_call_target="tpu_custom_call" | custom-call | tf_op jit(solution)/shard_map/total/pallas_call | solution.py:204
  (3 shorter events, 0.0 us)
Async XLA Ops:
  0.0 1.0 copy-start
  1.0 0.7 copy-start.7
  1.7 57.3 %copy-start.5 = (s32[12,7]{0,1:T(8,128)S(1)}, s32[12,7]{0,1:T(8,128)}, u32[]{:S(2)}) copy-start(s32[12,7]{0,1:T(8,128)} %param.7) | copy-start | bytes 1012
  1.7 57.3 %copy-start.6 = (s32[64,4]{0,1:T(4,128)S(1)}, s32[64,4]{0,1:T(4,128)}, u32[]{:S(2)}) copy-start(s32[64,4]{0,1:T(4,128)} %param.10) | copy-start | bytes 3076
  46.2 34.2 %all-to-all-start = ((bf16[64,64,128]{2,1,0:T(8,128)(2,1)}), bf16[64,64,128]{2,1,0:T(8,128)(2,1)S(1)}, u32[]{:S(2)}, u32[]{:S(2)}) async-start(bf16[64,64,128]{2,1,0:T(8,128)(2,1)} %get-tuple-element.14), calls=%async_computation | async-start | bytes 2097152 | tf_op jit(solution)/shard_map/all_to_all | solution.py:220
  51.6 1.0 copy-start.1
  52.6 1.1 copy-start.2
  53.7 0.7 copy-start.3
  54.4 33.1 %copy-start.4 = (s32[12,4]{0,1:T(4,128)S(1)}, s32[12,4]{0,1:T(4,128)}, u32[]{:S(2)}) copy-start(s32[12,4]{0,1:T(4,128)} %param.9) | copy-start | bytes 580
  80.4 23.6 %all-to-all-start.3 = ((bf16[8,64,512]{2,1,0:T(8,128)(2,1)}), bf16[8,64,512]{2,1,0:T(8,128)(2,1)S(1)}, u32[]{:S(2)}, u32[]{:S(2)}) async-start(bf16[8,64,512]{2,1,0:T(8,128)(2,1)} %bitcast.4), calls=%async_computation.3 | async-start | bytes 1048576 | tf_op jit(solution)/shard_map/all_to_all | solution.py:222

commit v2 on v0

v2 whole, which is shorter than its diff:
```python
import jax
import jax.numpy as jnp
from jax import lax
from jax.experimental import pallas as pl
from jax.experimental.pallas import tpu as pltpu
from jax.sharding import PartitionSpec as P

NC = 8
EXT = 8
PICKS = 4

NT = (((1,), (1,)), ((), ()))
NN = (((1,), (0,)), ((), ()))
MIB = 1024 * 1024
VMEM = pl.BlockSpec(memory_space=pltpu.VMEM)
SMEM = pl.BlockSpec(memory_space=pltpu.SMEM)
HBM = pl.BlockSpec(memory_space=pltpu.HBM)


def in_hbm(array):
    return pltpu.with_memory_space_constraint(array, pltpu.HBM)


def one_hot(condition):
    return condition.astype(jnp.float32).astype(jnp.bfloat16)


def pack_kernel(send_hbm, p_hbm, local_ref, sent_hbm, send_ref, p_ref, sems):
    rows, size, _ = p_ref.shape
    copies = [pltpu.make_async_copy(p_hbm, p_ref, sems.at[0]), pltpu.make_async_copy(send_hbm, send_ref, sems.at[1])]
    for copy in copies:
        copy.start()
    row = lax.broadcasted_iota(jnp.int32, (2 * size, PICKS * size), 0)
    col = lax.broadcasted_iota(jnp.int32, (2 * size, PICKS * size), 1)
    block = 2 * (row // size) * size + row % size
    lane = lax.broadcasted_iota(jnp.int32, (2 * size, 2 * size), 1)
    for copy in copies:
        copy.wait()
    flat = p_ref[...].reshape(rows * size, PICKS * size)
    turned = [
        lax.dot_general(one_hot(col == block + l * size), flat, NT, preferred_element_type=jnp.float32) for l in range(2)
    ]
    for u in range(rows // 2):
        low = turned[0][:, u * 2 * size : (u + 1) * 2 * size]
        high = turned[1][:, u * 2 * size : (u + 1) * 2 * size]
        local_ref[2 * u] = jnp.where(lane < size, low, pltpu.roll(high, size, 1)).astype(jnp.bfloat16)
        local_ref[2 * u + 1] = jnp.where(lane < size, pltpu.roll(low, size, 1), high).astype(jnp.bfloat16)
    moves = [
        pltpu.make_async_copy(local_ref.at[send_ref[s]], sent_hbm.at[s], sems.at[2]) for s in range(sent_hbm.shape[0])
    ]
    for move in moves:
        move.start()
    pltpu.make_async_copy(sent_hbm, sent_hbm, sems.at[2]).wait()


def pack(send_list, p_vals):
    rows, size, _ = p_vals.shape
    slots = send_list.shape[0]
    return pl.pallas_call(
        pack_kernel,
        out_shape=[
            pltpu.HBM((rows, 2 * size, 2 * size), p_vals.dtype),
            pltpu.HBM((slots, 2 * size, 2 * size), p_vals.dtype),
        ],
        in_specs=[HBM, HBM],
        out_specs=[VMEM, HBM],
        scratch_shapes=[
            pltpu.SMEM((slots,), jnp.int32),
            pltpu.VMEM(p_vals.shape, p_vals.dtype),
            pltpu.SemaphoreType.DMA((3,)),
        ],
        compiler_params=pltpu.CompilerParams(vmem_limit_bytes=8 * MIB),
        name="pack",
    )(in_hbm(send_list), in_hbm(p_vals))


def prepare_kernel(a_cols_ref, p_cols_ref, g_cols_ref, p_ref, a_ref, spread_ref, mixed_ref, start_ref, stacked):
    rows, size, _ = p_ref.shape
    width = a_ref.shape[2]
    links = width // size
    slots = g_cols_ref.shape[1]
    for b in range(links):
        for r in range(rows):
            e = a_cols_ref[b, r]
            near = jnp.minimum(e, rows - 1)
            far = jnp.clip(e - rows, 0, slots - 1)
            for k in range(PICKS):
                start_ref[b, rows * k + r] = size * jnp.where(e < rows, p_cols_ref[k, near], g_cols_ref[k, far])
    flat = p_ref[...].reshape(rows * size, PICKS * size)
    row = lax.broadcasted_iota(jnp.int32, (PICKS * size, PICKS * size), 0)
    col = lax.broadcasted_iota(jnp.int32, (PICKS * size, PICKS * size), 1)
    turned = lax.dot_general(one_hot(row == col), flat, NT, preferred_element_type=jnp.float32).astype(jnp.bfloat16)
    spread_ref[...] = jnp.zeros_like(spread_ref)
    for r in range(rows):
        for k in range(PICKS):
            start = pl.multiple_of(p_cols_ref[k, r] * size, size)
            spread_ref[pl.ds(start, size), r * size : (r + 1) * size] = turned[
                k * size : (k + 1) * size, r * size : (r + 1) * size
            ]
    for r in range(rows):
        for a in range(links):
            stacked[a * size : (a + 1) * size, r * size : (r + 1) * size] = a_ref[r, :, a * size : (a + 1) * size]
    row = lax.broadcasted_iota(jnp.int32, (width, width), 0)
    col = lax.broadcasted_iota(jnp.int32, (width, width), 1)
    pair = links * (row % size) + row // size
    moved = lax.dot_general(one_hot(col == pair), stacked[...], NN, preferred_element_type=jnp.float32).astype(jnp.bfloat16)
    for r in range(rows):
        part = moved[:, r * size : (r + 1) * size]
        mixed_ref[r] = jnp.concatenate([part, part], axis=1)


def prepare(a_cols, p_cols, gp_cols, p_vals, a_vals):
    rows, size, _ = p_vals.shape
    width = a_vals.shape[2]
    links = width // size
    return pl.pallas_call(
        prepare_kernel,
        out_shape=[
            pltpu.HBM((NC * size, rows * size), p_vals.dtype),
            pltpu.HBM((rows, width, 2 * size), p_vals.dtype),
            jax.ShapeDtypeStruct((links, PICKS * rows), jnp.int32),
        ],
        in_specs=[SMEM, SMEM, SMEM, VMEM, VMEM],
        out_specs=[VMEM, VMEM, SMEM],
        scratch_shapes=[pltpu.VMEM((width, rows * size), jnp.bfloat16)],
        compiler_params=pltpu.CompilerParams(vmem_limit_bytes=20 * MIB),
        name="prepare",
    )(a_cols.T, p_cols.T, gp_cols.T, p_vals, a_vals)


def product_kernel(a_cols_ref, start_ref, mixed_hbm, spread_hbm, local_hbm, ghost_ref, out_ref, mixed_ref, spread_ref, local_ref, placed, picked, terms, prod, sems, *sums):
    rows, width, double = mixed_ref.shape
    size = double // 2
    links = width // size
    slots = ghost_ref.shape[0]
    copies = [
        pltpu.make_async_copy(local_hbm, local_ref, sems.at[0]),
        pltpu.make_async_copy(mixed_hbm, mixed_ref, sems.at[1]),
        pltpu.make_async_copy(spread_hbm, spread_ref, sems.at[2]),
    ]
    for copy in copies:
        copy.start()
    for total in sums:
        total[...] = jnp.zeros_like(total)
    row = lax.broadcasted_iota(jnp.int32, (width, width), 0)
    col = lax.broadcasted_iota(jnp.int32, (width, width), 1)
    keep = one_hot(col // size == (links * (row % size) + row // size) // size)
    copies[0].wait()
    copies[1].wait()
    for r in range(rows):
        for a in range(links):
            e = a_cols_ref[a, r]
            near = local_ref[jnp.minimum(e, rows - 1)]
            far = ghost_ref[jnp.clip(e - rows, 0, slots - 1)]
            source = jnp.where(e < rows, near, far)
            for k in range(PICKS):
                h, l = divmod(k, 2)
                picked[r, k * size : (k + 1) * size, a * size : (a + 1) * size] = source[
                    h * size : (h + 1) * size, l * size : (l + 1) * size
                ]
        twice = mixed_ref[r]
        for t in range(0, width, double):
            stop = min(t + double, width)
            placed[r, :, t:stop] = twice[:, : stop - t] * keep[:, t:stop]
        terms[r] = lax.dot_general(picked[r], placed[r], NT, preferred_element_type=jnp.float32)
    for b in range(links):
        for k in range(PICKS):
            for odd in range(2):
                for u in range(rows // 2):
                    r = 2 * u + odd
                    here = pl.ds(pl.multiple_of(start_ref[b, rows * k + r], size), size)
                    lanes = slice(odd * size, (odd + 1) * size)
                    sums[u][here, lanes] = (
                        sums[u][here, lanes] + terms[r, k * size : (k + 1) * size, b * size : (b + 1) * size]
                    )
    for u in range(rows // 2):
        prod[:, 2 * u * size : 2 * (u + 1) * size] = sums[u][...].astype(jnp.bfloat16)
    copies[2].wait()
    out_ref[...] = lax.dot_general(
        spread_ref[...], prod[...], NT, preferred_element_type=jnp.float32
    ).astype(jnp.bfloat16)


def product(a_cols, start, mixed, spread, local, ghosts):
    rows, width, _ = mixed.shape
    size = local.shape[1] // 2
    wide = (NC + EXT) * size
    return pl.pallas_call(
        product_kernel,
        out_shape=jax.ShapeDtypeStruct((NC * size, wide), jnp.bfloat16),
        in_specs=[SMEM, SMEM, HBM, HBM, HBM, VMEM],
        out_specs=VMEM,
        scratch_shapes=[
            pltpu.VMEM(mixed.shape, jnp.bfloat16),
            pltpu.VMEM(spread.shape, jnp.bfloat16),
            pltpu.VMEM(local.shape, jnp.bfloat16),
            pltpu.VMEM((rows, width, width), jnp.bfloat16),
            pltpu.VMEM((rows, PICKS * size, width), jnp.bfloat16),
            pltpu.VMEM((rows, PICKS * size, width), jnp.float32),
            pltpu.VMEM((wide, rows * size), jnp.bfloat16),
            pltpu.SemaphoreType.DMA((3,)),
        ]
        + [pltpu.VMEM((wide, 2 * size), jnp.float32)] * (rows // 2),
        compiler_params=pltpu.CompilerParams(vmem_limit_bytes=32 * MIB),
        name="product",
    )(a_cols.T, start, in_hbm(mixed), in_hbm(spread), in_hbm(local), ghosts)


def total_kernel(part_ref, out_ref):
    total = part_ref[0].astype(jnp.float32)
    for c in range(1, part_ref.shape[0]):
        total = total + part_ref[c].astype(jnp.float32)
    out_ref[:, 0, :] = total


def total(parts):
    _, size, wide = parts.shape
    return pl.pallas_call(
        total_kernel,
        out_shape=jax.ShapeDtypeStruct((size, 1, wide), jnp.float32),
        in_specs=[VMEM],
        out_specs=VMEM,
        compiler_params=pltpu.CompilerParams(vmem_limit_bytes=8 * MIB),
        name="total",
    )(parts)


def on_device(a_vals, a_cols, p_vals, p_cols, gp_cols, send_list):
    size = p_vals.shape[1]
    local, outgoing = pack(send_list, p_vals)
    arrived = lax.all_to_all(outgoing, ("fine", "comp"), split_axis=0, concat_axis=0, tiled=True)
    spread, mixed, start = prepare(a_cols, p_cols, gp_cols, p_vals, a_vals)
    partial = product(a_cols, start, mixed, spread, local, arrived)
    moved = lax.all_to_all(partial, "coarse", split_axis=0, concat_axis=0, tiled=True)
    owned = total(moved.reshape(NC, size, -1))
    return owned.reshape((1, owned.shape[0], 1, owned.shape[2]))


def solution(mesh):
    placed = (
        P(("fine", "coarse", "comp"), None, None),
        P(("fine", "coarse", "comp"), None),
        P(("fine", "coarse", "comp"), None, None),
        P(("fine", "coarse", "comp"), None),
        P(("fine", "coarse", "comp"), None),
        P(("fine", "coarse", "comp")),
    )
    return jax.shard_map(
        on_device,
        mesh=mesh,
        in_specs=placed,
        out_specs=P("fine", "coarse", "comp", None),
        check_vma=False,
    )
```

time: 164 us -> 113 us (0.69)
  waiting for transfers between devices: 82.7 us -> 47.7 us
  blocking collectives: 0 us -> 34.7 us
  local copies, waits for them, and re-layouts: 27 us -> 0.03 us
  matrix products: 20.1 us -> 0 us
  Pallas kernels: 0 us -> 16 us
  between operations: 13.5 us -> 0.11 us
  other arithmetic: 5.9 us -> 0 us
    reduce_scatter x1 -> x0, waiting for transfers between devices: 40.6 us -> none  [on_device(): lax.psum_scatter(contract(spread, prod_rows), 'coarse', scatter_dimension...]
    all_to_all x0 -> x1, blocking collectives: none -> 34.7 us  [on_device(): lax.all_to_all(partial, 'coarse', split_axis=0, concat_axis=0, tiled=True)]
    dot_general x3 -> x0, matrix products: 20.1 us -> none  [the longest x1 10.6 us: local_terms(): jnp.einsum('rakc,riakj->ricj', placing, terms, precision=lax.Precision.HI...]
    reshape x5 -> x0, local copies, waits for them, and re-layouts: 17.4 us -> none  [the longest x1 10.1 us: local_terms(): terms.reshape(block_rows, block_size, link_count, pick_count, block_size)]
    pallas_call x0 -> x4, Pallas kernels: none -> 16 us  [the longest x1 7.98 us: product(): pl.pallas_call(product_kernel, out_shape=jax.ShapeDtypeStruct((NC * size,...]
    all_to_all x1, waiting for transfers between devices: 42.2 us -> 47.7 us  [on_device(): lax.all_to_all(outgoing, ('fine', 'comp'), split_axis=0, concat_axis=0, t...]
    gather x5 -> x0, local copies, waits for them, and re-layouts: 4.88 us -> none  [the longest x1 2.44 us: local_terms(): fetched = jnp.take(sources, a_index, axis=0)]
    select_n x5 -> x0, other arithmetic: 3.2 us -> none  [the longest x2 2.24 us: on_device(): outgoing = jnp.take(p_vals, send_list, axis=0)]
  transfers between devices with their start and end apart: 2 -> 1, of which waited for: 2 -> 1; matrix products, arithmetic and copies ran while one was open for 5% -> 0% of each run, Pallas kernels for 0% -> 3%
where the time goes in v2:
time: 113 us; the launch traced here: 112 us
  waiting for transfers between devices  47.7 us (42%)
  blocking collectives  34.7 us (31%)
  Pallas kernels  16 us (14%)
  starting transfers between devices  14 us (12%)
    all_to_all x1, waiting for transfers between devices, on_device(): lax.all_to_all(outgoing, ('fine', 'comp'), split_axis=0, concat_axis=0, t...  47.7 us
    all_to_all x1, blocking collectives, on_device(): lax.all_to_all(partial, 'coarse', split_axis=0, concat_axis=0, tiled=True)  34.7 us
    all_to_all x1, starting transfers between devices, on_device(): lax.all_to_all(outgoing, ('fine', 'comp'), split_axis=0, concat_axis=0, t...  14 us
    pallas_call x1, Pallas kernels, product(): pl.pallas_call(product_kernel, out_shape=jax.ShapeDtypeStruct((NC * size,...  7.98 us
    pallas_call x1, Pallas kernels, pack(): pl.pallas_call(pack_kernel, out_shape=[pltpu.HBM((rows, 2 * size, 2 * siz...  3.62 us
    pallas_call x1, Pallas kernels, prepare(): pl.pallas_call(prepare_kernel, out_shape=[pltpu.HBM((NC * size, rows * si...  3.54 us
  transfers between devices with their start and end apart: 1, of which 1 were waited for; matrix products, arithmetic and copies ran while one was open for 0% of the time, Pallas kernels for 3%

profile of v2, /device:TPU:6, one launch (start us, length us, event | category | flops | bytes accessed | tf_op | source)
XLA Modules:
  0.0 112.5 jit_solution(4851442670161447617)
XLA Ops:
  0.0 3.6 %pack.1 = (bf16[12,128,128]{2,1,0:T(8,128)(2,1)}, bf16[64,128,128]{2,1,0:T(8,128)(2,1)}) custom-call(s32[64]{0:T(128)} %send_hbm.1, bf16[12,64,256]{2,1,0:T(8,128)(2,1)} %p_hbm.1), custom_call_target="tpu_custom_call" | custom-call | tf_op jit(solution)/shard_map/pack/pallas_call | solution.py:59
  3.6 0.0 copy-start
  3.6 0.0 copy-start.1
  3.6 0.0 copy-start.2
  3.7 0.0 copy-start.3
  3.7 0.0 copy-start.4
  3.7 14.0 %all-to-all-start = ((bf16[64,128,128]{2,1,0:T(8,128)(2,1)}), bf16[64,128,128]{2,1,0:T(8,128)(2,1)S(1)}, u32[]{:S(2)}, u32[]{:S(2)}) async-start(bf16[64,128,128]{2,1,0:T(8,128)(2,1)} %get-tuple-element.14), calls=%async_computation | async-start | bytes 4194304 | tf_op jit(solution)/shard_map/all_to_all | solution.py:231
  17.6 0.0 copy-done
  17.7 0.0 copy-done.1
  17.7 0.0 copy-done.2
  17.7 0.0 copy-done.3
  17.7 0.0 copy-done.4
  17.7 3.5 %prepare.1 = (bf16[512,768]{1,0:T(8,128)(2,1)}, bf16[12,448,128]{2,1,0:T(8,128)(2,1)}, s32[7,48]{1,0:T(8,128)S(1)}) custom-call(s32[7,12]{1,0:T(8,128)S(1)} %bitcast.6, s32[4,12]{1,0:T(4,128)S(1)} %bitcast.8, s32[4,64]{1,0:T(4,128)S(1)} %bitcast.9, bf16[12,64,256]{2,1,0:T(8,128)(2,1)S(1)} %copy-done, bf16[12,64,448]{2,1,0:T(8,128)(2,1)S(1)} %copy-done.1), custom_call_target="tpu_custom_call" | custom-call | tf_op jit(solution)/shard_map/prepare/pallas_call | solution.py:116
  21.2 47.7 %all-to-all-done.ghost_ref = bf16[64,128,128]{2,1,0:T(8,128)(2,1)S(1)} async-done(((bf16[64,128,128]{2,1,0:T(8,128)(2,1)}), bf16[64,128,128]{2,1,0:T(8,128)(2,1)S(1)}, u32[]{:S(2)}, u32[]{:S(2)}) %all-to-all-start) | async-done | bytes 2097184 | tf_op jit(solution)/shard_map/all_to_all | solution.py:231
  68.9 8.0 %product.1 = bf16[512,1024]{1,0:T(8,128)(2,1)S(1)} custom-call(s32[7,12]{1,0:T(8,128)S(1)} %bitcast.7, s32[7,48]{1,0:T(8,128)S(1)} %get-tuple-element.10.start_ref, bf16[12,448,128]{2,1,0:T(8,128)(2,1)} %get-tuple-element.11.mixed_hbm, bf16[512,768]{1,0:T(8,128)(2,1)} %get-tuple-element.12.spread_hbm, bf16[12,128,128]{2,1,0:T(8,128)(2,1)} %get-tuple-element.13.local_hbm, ...), custom_call_target="tpu_custom_call" | custom-call | tf_op jit(solution)/shard_map/product/pallas_call | solution.py:188
  76.9 34.7 %all_to_all.14.part_ref = bf16[8,64,1024]{2,1,0:T(8,128)(2,1)S(1)} all-to-all(bf16[8,64,1024]{2,1,0:T(8,128)(2,1)S(1)} %bitcast.5), channel_id=1, replica_groups=mesh['fine'=16,'coarse'=8,'comp'=4] {'coarse'}, dimensions={0} | all-to-all | bytes 2097152 | tf_op jit(solution)/shard_map/all_to_all | solution.py:234
  111.6 0.9 total.1
Async XLA Ops:
  3.6 14.0 %copy-start = (bf16[12,64,256]{2,1,0:T(8,128)(2,1)S(1)}, bf16[12,64,256]{2,1,0:T(8,128)(2,1)}, u32[]{:S(2)}) copy-start(bf16[12,64,256]{2,1,0:T(8,128)(2,1)} %p_hbm.1) | copy-start | bytes 1179652
  3.6 14.0 %copy-start.1 = (bf16[12,64,448]{2,1,0:T(8,128)(2,1)S(1)}, bf16[12,64,448]{2,1,0:T(8,128)(2,1)}, u32[]{:S(2)}) copy-start(bf16[12,64,448]{2,1,0:T(8,128)(2,1)} %a_ref.1) | copy-start | bytes 2064388
  3.6 14.0 %copy-start.2 = (s32[12,7]{0,1:T(8,128)S(1)}, s32[12,7]{0,1:T(8,128)}, u32[]{:S(2)}) copy-start(s32[12,7]{0,1:T(8,128)} %param.7) | copy-start | bytes 1012
  3.7 14.0 %copy-start.3 = (s32[12,4]{0,1:T(4,128)S(1)}, s32[12,4]{0,1:T(4,128)}, u32[]{:S(2)}) copy-start(s32[12,4]{0,1:T(4,128)} %param.9) | copy-start | bytes 580
  3.7 14.0 %copy-start.4 = (s32[64,4]{0,1:T(4,128)S(1)}, s32[64,4]{0,1:T(4,128)}, u32[]{:S(2)}) copy-start(s32[64,4]{0,1:T(4,128)} %param.10) | copy-start | bytes 3076
  3.7 65.2 %all-to-all-start = ((bf16[64,128,128]{2,1,0:T(8,128)(2,1)}), bf16[64,128,128]{2,1,0:T(8,128)(2,1)S(1)}, u32[]{:S(2)}, u32[]{:S(2)}) async-start(bf16[64,128,128]{2,1,0:T(8,128)(2,1)} %get-tuple-element.14), calls=%async_computation | async-start | bytes 4194304 | tf_op jit(solution)/shard_map/all_to_all | solution.py:231

commit v3 on v2

v3 whole, which is shorter than its diff:
```python
import jax
import jax.numpy as jnp
from jax import lax
from jax.experimental import pallas as pl
from jax.experimental.pallas import tpu as pltpu
from jax.sharding import Mesh
from jax.sharding import PartitionSpec as P

NC = 8
EXT = 8
PICKS = 4

NT = (((1,), (1,)), ((), ()))
NN = (((1,), (0,)), ((), ()))
MIB = 1024 * 1024
VMEM = pl.BlockSpec(memory_space=pltpu.VMEM)
SMEM = pl.BlockSpec(memory_space=pltpu.SMEM)
HBM = pl.BlockSpec(memory_space=pltpu.HBM)


def in_hbm(array):
    return pltpu.with_memory_space_constraint(array, pltpu.HBM)


def one_hot(condition):
    return condition.astype(jnp.float32).astype(jnp.bfloat16)


def pack_kernel(send_hbm, p_hbm, sent_hbm, send_ref, p_ref, packed_ref, sems):
    rows, size, _ = p_ref.shape
    w = size // 2
    copies = [pltpu.make_async_copy(p_hbm, p_ref, sems.at[0]), pltpu.make_async_copy(send_hbm, send_ref, sems.at[1])]
    for copy in copies:
        copy.start()
    row = lax.broadcasted_iota(jnp.int32, (2 * size, PICKS * size), 0)
    col = lax.broadcasted_iota(jnp.int32, (2 * size, PICKS * size), 1)
    block = 2 * (row % size // w) * size + row // size * w + row % w
    lane = lax.broadcasted_iota(jnp.int32, (2 * size, 2 * size), 1)
    picks = [one_hot(col == block + l * size) for l in range(2)]
    for copy in copies:
        copy.wait()
    flat = p_ref[...].reshape(rows * size, PICKS * size)
    turned = [lax.dot_general(pick, flat, NT, preferred_element_type=jnp.float32) for pick in picks]
    for u in range(rows // 2):
        low = turned[0][:, u * 2 * size : (u + 1) * 2 * size]
        high = turned[1][:, u * 2 * size : (u + 1) * 2 * size]
        even = jnp.where(lane < size, low, pltpu.roll(high, size, 1)).astype(jnp.bfloat16)
        odd = jnp.where(lane < size, pltpu.roll(low, size, 1), high).astype(jnp.bfloat16)
        for d in range(2):
            packed_ref[2 * u, d] = even[d * size : (d + 1) * size]
            packed_ref[2 * u + 1, d] = odd[d * size : (d + 1) * size]
    moves = []
    for f in range(sent_hbm.shape[0]):
        for m in range(sent_hbm.shape[2]):
            slot = f * sent_hbm.shape[2] + m
            moves.append(pltpu.make_async_copy(packed_ref.at[send_ref[slot]], sent_hbm.at[f, :, m], sems.at[2]))
    for move in moves:
        move.start()
    pltpu.make_async_copy(sent_hbm, sent_hbm, sems.at[2]).wait()


def pack(send_list, p_vals, comp):
    rows, size, _ = p_vals.shape
    slots = send_list.shape[0]
    return pl.pallas_call(
        pack_kernel,
        out_shape=pltpu.HBM((slots // comp, 2, comp, size, 2 * size), p_vals.dtype),
        in_specs=[HBM, HBM],
        out_specs=HBM,
        scratch_shapes=[
            pltpu.SMEM((slots,), jnp.int32),
            pltpu.VMEM(p_vals.shape, p_vals.dtype),
            pltpu.VMEM((rows, 2, size, 2 * size), p_vals.dtype),
            pltpu.SemaphoreType.DMA((3,)),
        ],
        compiler_params=pltpu.CompilerParams(vmem_limit_bytes=8 * MIB),
        name="pack",
    )(in_hbm(send_list), in_hbm(p_vals))


def prepare_kernel(links, comp, where_ref, tables_ref, p_ref, a_ref, spread_ref, mixed_ref, local_ref, start_ref, source_ref, stacked):
    rows, size, _ = p_ref.shape
    width = a_ref.shape[2]
    w = size // 2
    slots = tables_ref.shape[1]
    half = where_ref[0]
    place = where_ref[1]
    for b in range(links):
        for r in range(rows):
            e = tables_ref[b, r]
            near = jnp.minimum(e, rows - 1)
            far = jnp.clip(e - rows, 0, slots - 1)
            arrived = rows + (2 * (far // comp) + place) * comp + far % comp
            source_ref[b, r] = jnp.where(e < rows, near, arrived)
            for k in range(PICKS):
                c = jnp.where(e < rows, tables_ref[links + k, near], tables_ref[links + PICKS + k, far])
                spot = c // 4 * 4 + c % 2 * 2 + jnp.where(half == 0, c // 2 % 2, 1 - c // 2 % 2)
                start_ref[b, rows * k + r] = spot * w
    flat = p_ref[...].reshape(rows * size, PICKS * size)
    row = lax.broadcasted_iota(jnp.int32, (PICKS * size, PICKS * size), 0)
    col = lax.broadcasted_iota(jnp.int32, (PICKS * size, PICKS * size), 1)
    turned = lax.dot_general(one_hot(row == col), flat, NT, preferred_element_type=jnp.float32).astype(jnp.bfloat16)
    spread_ref[...] = jnp.zeros_like(spread_ref)
    for r in range(rows):
        for k in range(PICKS):
            start = pl.multiple_of(tables_ref[links + k, r] * size, size)
            spread_ref[pl.ds(start, size), r * size : (r + 1) * size] = turned[
                k * size : (k + 1) * size, r * size : (r + 1) * size
            ]
    row = lax.broadcasted_iota(jnp.int32, (size, PICKS * size), 0)
    col = lax.broadcasted_iota(jnp.int32, (size, PICKS * size), 1)
    block = 2 * (row // w) * size + half * w + row % w
    lane = lax.broadcasted_iota(jnp.int32, (size, 2 * size), 1)
    packed = [
        lax.dot_general(one_hot(col == block + l * size), flat, NT, preferred_element_type=jnp.float32) for l in range(2)
    ]
    for u in range(rows // 2):
        low = packed[0][:, u * 2 * size : (u + 1) * 2 * size]
        high = packed[1][:, u * 2 * size : (u + 1) * 2 * size]
        local_ref[2 * u] = jnp.where(lane < size, low, pltpu.roll(high, size, 1)).astype(jnp.bfloat16)
        local_ref[2 * u + 1] = jnp.where(lane < size, pltpu.roll(low, size, 1), high).astype(jnp.bfloat16)
    for r in range(rows):
        for a in range(links):
            stacked[a * size : (a + 1) * size, r * size : (r + 1) * size] = a_ref[r, :, a * size : (a + 1) * size]
    row = lax.broadcasted_iota(jnp.int32, (width, width), 0)
    col = lax.broadcasted_iota(jnp.int32, (width, width), 1)
    pair = links * (row % size) + row // size
    moved = lax.dot_general(one_hot(col == pair), stacked[...], NN, preferred_element_type=jnp.float32).astype(jnp.bfloat16)
    for r in range(rows):
        part = moved[:, r * size : (r + 1) * size]
        mixed_ref[r] = jnp.concatenate([part, part], axis=1)


def prepare(comp, where, tables, p_vals, a_vals):
    rows, size, _ = p_vals.shape
    width = a_vals.shape[2]
    links = width // size
    return pl.pallas_call(
        lambda *refs: prepare_kernel(links, comp, *refs),
        out_shape=[
            pltpu.HBM((NC * size, rows * size), p_vals.dtype),
            pltpu.HBM((rows, width, 2 * size), p_vals.dtype),
            pltpu.HBM((rows, size, 2 * size), p_vals.dtype),
            jax.ShapeDtypeStruct((links, PICKS * rows), jnp.int32),
            jax.ShapeDtypeStruct((links, rows), jnp.int32),
        ],
        in_specs=[SMEM, SMEM, VMEM, VMEM],
        out_specs=[VMEM, VMEM, VMEM, SMEM, SMEM],
        scratch_shapes=[pltpu.VMEM((width, rows * size), jnp.bfloat16)],
        compiler_params=pltpu.CompilerParams(vmem_limit_bytes=20 * MIB),
        name="prepare",
    )(where, tables, p_vals, a_vals)


def product_kernel(*refs):
    starts, sources, spreads_hbm, mixed_hbm, local_hbm = (refs[i : i + 2] for i in range(0, 10, 2))
    ghost_ref, out_ref, spread_ref, mixed_ref, local_ref, placed, picked, terms, prod, sems = refs[10:20]
    sums = refs[20:]
    _, rows, width, double = mixed_ref.shape
    size = double // 2
    w = size // 2
    links = width // size
    slots = ghost_ref.shape[0]
    copies = []
    for n, (here, there) in enumerate(((local_hbm, local_ref), (mixed_hbm, mixed_ref), (spreads_hbm, spread_ref))):
        for o in range(2):
            copies.append(pltpu.make_async_copy(here[o], there.at[o], sems.at[2 * n + o]))
    for copy in copies:
        copy.start()
    for total in sums:
        total[...] = jnp.zeros_like(total)
    row = lax.broadcasted_iota(jnp.int32, (width, width), 0)
    col = lax.broadcasted_iota(jnp.int32, (width, width), 1)
    keep = one_hot(col // size == (links * (row % size) + row // size) // size)
    for copy in copies[:4]:
        copy.wait()
    for o in range(2):
        for r in range(rows):
            q = o * rows + r
            for a in range(links):
                e = sources[o][a, r]
                near = local_ref[o, jnp.minimum(e, rows - 1)]
                far = ghost_ref[jnp.clip(e - rows, 0, slots - 1)]
                source = jnp.where(e < rows, near, far)
                for k in range(PICKS):
                    h, l = divmod(k, 2)
                    picked[q, k * w : (k + 1) * w, a * size : (a + 1) * size] = source[
                        h * w : (h + 1) * w, l * size : (l + 1) * size
                    ]
            twice = mixed_ref[o, r]
            for t in range(0, width, double):
                stop = min(t + double, width)
                placed[q, :, t:stop] = twice[:, : stop - t] * keep[:, t:stop]
            terms[q] = lax.dot_general(picked[q], placed[q], NT, preferred_element_type=jnp.float32)
    for b in range(links):
        for k in range(PICKS):
            for odd in range(2):
                for u in range(rows):
                    o, r = divmod(2 * u + odd, rows)
                    here = pl.ds(pl.multiple_of(starts[o][b, rows * k + r], w), w)
                    lanes = slice(odd * size, (odd + 1) * size)
                    sums[u][here, lanes] = (
                        sums[u][here, lanes] + terms[2 * u + odd, k * w : (k + 1) * w, b * size : (b + 1) * size]
                    )
    for u in range(rows):
        prod[:, u * double : (u + 1) * double] = sums[u][...].astype(jnp.bfloat16)
    for copy in copies[4:]:
        copy.wait()
    whole = rows * size
    out_ref[...] = (
        lax.dot_general(spread_ref[0], prod[:, :whole], NT, preferred_element_type=jnp.float32)
        + lax.dot_general(spread_ref[1], prod[:, whole:], NT, preferred_element_type=jnp.float32)
    ).astype(jnp.bfloat16)


def product(mine, other, ghosts):
    spread, mixed, local, _, _ = mine
    rows, width, double = mixed.shape
    size = double // 2
    wide = (NC + EXT) * (size // 2)
    operands = []
    for n in (3, 4):
        operands += [mine[n], other[n]]
    for n in (0, 1, 2):
        operands += [in_hbm(mine[n]), in_hbm(other[n])]
    return pl.pallas_call(
        product_kernel,
        out_shape=jax.ShapeDtypeStruct((NC * size, wide), jnp.bfloat16),
        in_specs=[SMEM] * 4 + [HBM] * 6 + [VMEM],
        out_specs=VMEM,
        scratch_shapes=[
            pltpu.VMEM((2, *spread.shape), jnp.bfloat16),
            pltpu.VMEM((2, *mixed.shape), jnp.bfloat16),
            pltpu.VMEM((2, *local.shape), jnp.bfloat16),
            pltpu.VMEM((2 * rows, width, width), jnp.bfloat16),
            pltpu.VMEM((2 * rows, 2 * size, width), jnp.bfloat16),
            pltpu.VMEM((2 * rows, 2 * size, width), jnp.float32),
            pltpu.VMEM((wide, 2 * rows * size), jnp.bfloat16),
            pltpu.SemaphoreType.DMA((6,)),
        ]
        + [pltpu.VMEM((wide, double), jnp.float32)] * rows,
        compiler_params=pltpu.CompilerParams(vmem_limit_bytes=44 * MIB),
        name="product",
    )(*operands, ghosts)


def total_kernel(part_ref, out_ref):
    parts, size, wide = part_ref.shape
    halves = []
    for d in range(2):
        total = part_ref[d].astype(jnp.float32)
        for c in range(d + 2, parts, 2):
            total = total + part_ref[c].astype(jnp.float32)
        halves.append(total)
    group = 2 * size
    first = lax.broadcasted_iota(jnp.int32, (size, group), 1) // (size // 2) % 2 == 0
    for u in range(wide // group):
        low = halves[0][:, u * group : (u + 1) * group]
        high = halves[1][:, u * group : (u + 1) * group]
        out_ref[:, 0, 2 * u * group : (2 * u + 1) * group] = jnp.where(first, low, high)
        out_ref[:, 0, (2 * u + 1) * group : (2 * u + 2) * group] = jnp.where(
            first, pltpu.roll(low, group - size // 2, 1), pltpu.roll(high, size // 2, 1)
        )


def total(parts):
    _, size, wide = parts.shape
    return pl.pallas_call(
        total_kernel,
        out_shape=jax.ShapeDtypeStruct((size, 1, 2 * wide), jnp.float32),
        in_specs=[VMEM],
        out_specs=VMEM,
        compiler_params=pltpu.CompilerParams(vmem_limit_bytes=8 * MIB),
        name="total",
    )(parts)


def on_device(a_vals, a_cols, p_vals, p_cols, gp_cols, send_list):
    size = p_vals.shape[1]
    slots = send_list.shape[0]
    comp = lax.axis_size("comp")
    outgoing = pack(send_list, p_vals, comp)
    outgoing = outgoing.reshape(-1, *outgoing.shape[3:])
    arrived = lax.all_to_all(outgoing, ("fine", "inner", "comp"), split_axis=0, concat_axis=0, tiled=True)
    half = lax.axis_index("inner")
    columns = [jnp.pad(table.T, ((0, 0), (0, slots - table.shape[0]))) for table in (a_cols, p_cols, gp_cols)]
    tables = jnp.concatenate(columns, axis=0)
    swap = ((0, 1), (1, 0))
    a_other, p_other, tables_other = (lax.ppermute(array, "inner", swap) for array in (a_vals, p_vals, tables))
    mine = prepare(comp, jnp.stack([half, half]), tables, p_vals, a_vals)
    other = prepare(comp, jnp.stack([half, 1 - half]), tables_other, p_other, a_other)
    partial = product(mine, other, arrived)
    moved = lax.all_to_all(partial, ("outer", "inner"), split_axis=0, concat_axis=0, tiled=True)
    owned = total(moved.reshape(NC, size, -1))
    return owned.reshape((1, owned.shape[0], 1, owned.shape[2]))


def solution(mesh):
    fine, coarse, comp = mesh.devices.shape
    pairs = Mesh(mesh.devices.reshape(fine, coarse // 2, 2, comp), ("fine", "outer", "inner", "comp"))
    rows = ("fine", "outer", "inner", "comp")
    placed = (
        P(rows, None, None),
        P(rows, None),
        P(rows, None, None),
        P(rows, None),
        P(rows, None),
        P(rows),
    )
    return jax.shard_map(
        on_device,
        mesh=pairs,
        in_specs=placed,
        out_specs=P("fine", ("outer", "inner"), "comp", None),
        check_vma=False,
    )
```

time: 113 us -> 113 us (level)
  waiting for transfers between devices: 47.7 us -> 31.9 us
  Pallas kernels: 16 us -> 31.5 us
  blocking collectives: 34.7 us -> 23.4 us
  starting transfers between devices: 14 us -> 25.1 us
    all_to_all x1, waiting for transfers between devices: 47.7 us -> 0.01 us  [on_device(): lax.all_to_all(outgoing, ('fine', 'inner', 'comp'), split_axis=0, concat_...]
    ppermute x0 -> x3, waiting for transfers between devices: none -> 31.9 us  [on_device(): lax.ppermute(array, 'inner', swap)]
    pallas_call x3 -> x4, Pallas kernels: 8.03 us -> 21 us  [the longest x2 17.2 us: prepare(): pl.pallas_call(lambda *refs: prepare_kernel(links, comp, *refs), out_shap...]
    all_to_all x1, blocking collectives: 34.7 us -> 23.4 us  [on_device(): lax.all_to_all(partial, ('outer', 'inner'), split_axis=0, concat_axis=0,...]
    ppermute x0 -> x3, starting transfers between devices: none -> 9.4 us  [on_device(): lax.ppermute(array, 'inner', swap)]
    pallas_call x1, Pallas kernels: 7.98 us -> 10.5 us  [product(): pl.pallas_call(product_kernel, out_shape=jax.ShapeDtypeStruct((NC * size,...]
    all_to_all x1, starting transfers between devices: 14 us -> 15.8 us  [on_device(): lax.all_to_all(outgoing, ('fine', 'inner', 'comp'), split_axis=0, concat_...]
  transfers between devices with their start and end apart: 1 -> 4, of which waited for: 1 -> 1; matrix products, arithmetic and copies ran while one was open for 0% -> 0% of each run, Pallas kernels for 3% -> 15%
where the time goes in v3:
time: 113 us; the launch traced here: 112 us
  waiting for transfers between devices  31.9 us (28%)
  Pallas kernels  31.5 us (28%)
  starting transfers between devices  25.1 us (22%)
  blocking collectives  23.4 us (21%)
    ppermute x3, waiting for transfers between devices, on_device(): lax.ppermute(array, 'inner', swap)  31.9 us
    all_to_all x1, blocking collectives, on_device(): lax.all_to_all(partial, ('outer', 'inner'), split_axis=0, concat_axis=0,...  23.4 us
    pallas_call x2, Pallas kernels, prepare(): pl.pallas_call(lambda *refs: prepare_kernel(links, comp, *refs), out_shap...  17.2 us
    all_to_all x1, starting transfers between devices, on_device(): lax.all_to_all(outgoing, ('fine', 'inner', 'comp'), split_axis=0, concat_...  15.8 us
    pallas_call x1, Pallas kernels, product(): pl.pallas_call(product_kernel, out_shape=jax.ShapeDtypeStruct((NC * size,...  10.5 us
    ppermute x3, starting transfers between devices, on_device(): lax.ppermute(array, 'inner', swap)  9.4 us
    pallas_call x1, Pallas kernels, pack(): pl.pallas_call(pack_kernel, out_shape=pltpu.HBM((slots // comp, 2, comp,...  2.83 us
  transfers between devices with their start and end apart: 4, of which 1 were waited for; matrix products, arithmetic and copies ran while one was open for 0% of the time, Pallas kernels for 15%

profile of v3, /device:TPU:6, one launch (start us, length us, event | category | flops | bytes accessed | tf_op | source)
XLA Modules:
  0.0 112.3 jit_solution(17079622940603747589)
XLA Ops:
  0.0 2.8 %pack.1 = bf16[16,2,4,64,128]{4,3,2,1,0:T(8,128)(2,1)} custom-call(s32[64]{0:T(128)} %send_hbm.1, bf16[12,64,256]{2,1,0:T(8,128)(2,1)} %p_hbm.1), custom_call_target="tpu_custom_call" | custom-call | tf_op jit(solution)/shard_map/pack/pallas_call | solution.py:65
  2.8 0.0 copy-start.1
  2.9 0.0 copy-start
  2.9 0.0 copy-start.2
  2.9 0.0 copy-start.3
  2.9 0.0 copy-start.4
  2.9 15.8 %all-to-all-start = ((bf16[128,64,128]{2,1,0:T(8,128)(2,1)}), bf16[128,64,128]{2,1,0:T(8,128)(2,1)S(1)}, u32[]{:S(2)}, u32[]{:S(2)}) async-start(bf16[128,64,128]{2,1,0:T(8,128)(2,1)} %bitcast.9), calls=%async_computation | async-start | bytes 4194304 | tf_op jit(solution)/shard_map/all_to_all | solution.py:284
  18.7 3.4 %collective-permute-start.2 = (bf16[12,64,448]{2,1,0:T(8,128)(2,1)S(1)}, bf16[12,64,448]{2,1,0:T(8,128)(2,1)}, u32[]{:S(2)}, u32[]{:S(2)}) collective-permute-start(bf16[12,64,448]{2,1,0:T(8,128)(2,1)S(1)} %copy-done.1), channel_id=1, source_target_pairs={{0,4},{4,0},{1,5},{5,1},{2,6},{6,2},{3,7},{7,3},{8,12},{12,8},{9,1... | collective-permute-start | bytes 2064392 | tf_op jit(solution)/shard_map/ppermute | solution.py:289
  22.0 0.0 copy-done
  22.1 2.5 %collective-permute-start.1 = (bf16[12,64,256]{2,1,0:T(8,128)(2,1)S(1)}, bf16[12,64,256]{2,1,0:T(8,128)(2,1)}, u32[]{:S(2)}, u32[]{:S(2)}) collective-permute-start(bf16[12,64,256]{2,1,0:T(8,128)(2,1)S(1)} %copy-done), channel_id=1, source_target_pairs={{0,4},{4,0},{1,5},{5,1},{2,6},{6,2},{3,7},{7,3},{8,12},{12,8},{9,1... | collective-permute-start | bytes 1179656 | tf_op jit(solution)/shard_map/ppermute | solution.py:289
  24.5 0.0 copy-done.2
  24.5 0.0 copy-done.3
  24.6 3.6 %collective-permute-start = (s32[15,64]{1,0:T(8,128)S(1)}, s32[15,64]{1,0:T(8,128)S(1)}, u32[]{:S(2)}, u32[]{:S(2)}) collective-permute-start(s32[15,64]{1,0:T(8,128)S(1)} %fusion.refs_1_), channel_id=1, source_target_pairs={{0,4},{4,0},{1,5},{5,1},{2,6},{6,2},{3,7},{7,3},{8,12},{12,8},{9,1... | collective-permute-start | bytes 11528 | tf_op jit(solution)/shard_map/ppermute | solution.py:289
  28.1 0.1 pad_add_fusion.1.refs_0_
  28.2 0.1 pad_add_fusion.2.refs_0_
  28.3 8.2 %prepare.2 = (bf16[512,768]{1,0:T(8,128)(2,1)}, bf16[12,448,128]{2,1,0:T(8,128)(2,1)}, bf16[12,64,128]{2,1,0:T(8,128)(2,1)}, s32[7,48]{1,0:T(8,128)S(1)}, s32[7,12]{1,0:T(8,128)S(1)}) custom-call(s32[2]{0:T(128)S(1)} %pad_add_fusion.1.refs_0_, s32[15,64]{1,0:T(8,128)S(1)} %fusion.refs_1_, bf16[12,64,256]{2,1,0:T(8,128)(2,1)S(1)} %copy-done, ...), custom_call_target="tpu_custom_call" | custom-call | tf_op jit(solution)/shard_map/prepare/pallas_call | solution.py:138
  36.5 31.9 %collective-permute-done.refs_1_ = s32[15,64]{1,0:T(8,128)S(1)} collective-permute-done((s32[15,64]{1,0:T(8,128)S(1)}, s32[15,64]{1,0:T(8,128)S(1)}, u32[]{:S(2)}, u32[]{:S(2)}) %collective-permute-start) | collective-permute-done | bytes 3872 | tf_op jit(solution)/shard_map/ppermute | solution.py:289
  68.4 0.0 collective-permute-done.1.refs_2_
  68.4 0.0 collective-permute-done.2.refs_3_
  68.4 9.0 %prepare.3 = (bf16[512,768]{1,0:T(8,128)(2,1)}, bf16[12,448,128]{2,1,0:T(8,128)(2,1)}, bf16[12,64,128]{2,1,0:T(8,128)(2,1)}, s32[7,48]{1,0:T(8,128)S(1)}, s32[7,12]{1,0:T(8,128)S(1)}) custom-call(s32[2]{0:T(128)S(1)} %pad_add_fusion.2.refs_0_, s32[15,64]{1,0:T(8,128)S(1)} %collective-permute-done.refs_1_, ...), custom_call_target="tpu_custom_call" | custom-call | tf_op jit(solution)/shard_map/prepare/pallas_call | solution.py:138
  77.4 0.0 all-to-all-done.refs_10_
  77.5 10.5 %product.1 = bf16[512,512]{1,0:T(8,128)(2,1)S(1)} custom-call(s32[7,48]{1,0:T(8,128)S(1)} %get-tuple-element.15.refs_0_, s32[7,48]{1,0:T(8,128)S(1)} %get-tuple-element.16.refs_1_, s32[7,12]{1,0:T(8,128)S(1)} %get-tuple-element.17.refs_2_, s32[7,12]{1,0:T(8,128)S(1)} %get-tuple-element.18.refs_3_, bf16[512,768]{1,0:T(8,128)(2,1)} %get-tuple-element.19.refs_4_, ...), custom_call_target="tpu_custom_call" | custom-call | tf_op jit(solution)/shard_map/product/pallas_call | solution.py:226
  88.0 23.4 %all_to_all.14.part_ref = bf16[8,64,512]{2,1,0:T(8,128)(2,1)S(1)} all-to-all(bf16[8,64,512]{2,1,0:T(8,128)(2,1)S(1)} %bitcast.8), channel_id=1, replica_groups=mesh['fine'=16,'outer'=4,'inner'=2,'comp'=4] {'outer','inner'}, dimensions={0} | all-to-all | bytes 1048576 | tf_op jit(solution)/shard_map/all_to_all | solution.py:293
  111.4 0.9 total.1
  (3 shorter events, 0.0 us)
Async XLA Ops:
  2.8 15.8 %copy-start.1 = (bf16[12,64,448]{2,1,0:T(8,128)(2,1)S(1)}, bf16[12,64,448]{2,1,0:T(8,128)(2,1)}, u32[]{:S(2)}) copy-start(bf16[12,64,448]{2,1,0:T(8,128)(2,1)} %refs_3_.1) | copy-start | bytes 2064388
  2.9 19.2 %copy-start = (bf16[12,64,256]{2,1,0:T(8,128)(2,1)S(1)}, bf16[12,64,256]{2,1,0:T(8,128)(2,1)}, u32[]{:S(2)}) copy-start(bf16[12,64,256]{2,1,0:T(8,128)(2,1)} %p_hbm.1) | copy-start | bytes 1179652
  2.9 21.7 %copy-start.2 = (s32[12,7]{0,1:T(8,128)S(1)}, s32[12,7]{0,1:T(8,128)}, u32[]{:S(2)}) copy-start(s32[12,7]{0,1:T(8,128)} %param.7) | copy-start | bytes 1012
  2.9 21.7 %copy-start.3 = (s32[12,4]{0,1:T(4,128)S(1)}, s32[12,4]{0,1:T(4,128)}, u32[]{:S(2)}) copy-start(s32[12,4]{0,1:T(4,128)} %param.9) | copy-start | bytes 580
  2.9 21.7 %copy-start.4 = (s32[64,4]{0,1:T(4,128)S(1)}, s32[64,4]{0,1:T(4,128)}, u32[]{:S(2)}) copy-start(s32[64,4]{0,1:T(4,128)} %param.10) | copy-start | bytes 3076
  2.9 74.6 %all-to-all-start = ((bf16[128,64,128]{2,1,0:T(8,128)(2,1)}), bf16[128,64,128]{2,1,0:T(8,128)(2,1)S(1)}, u32[]{:S(2)}, u32[]{:S(2)}) async-start(bf16[128,64,128]{2,1,0:T(8,128)(2,1)} %bitcast.9), calls=%async_computation | async-start | bytes 4194304 | tf_op jit(solution)/shard_map/all_to_all | solution.py:284
  18.7 49.7 %collective-permute-start.2 = (bf16[12,64,448]{2,1,0:T(8,128)(2,1)S(1)}, bf16[12,64,448]{2,1,0:T(8,128)(2,1)}, u32[]{:S(2)}, u32[]{:S(2)}) collective-permute-start(bf16[12,64,448]{2,1,0:T(8,128)(2,1)S(1)} %copy-done.1), channel_id=1, source_target_pairs={{0,4},{4,0},{1,5},{5,1},{2,6},{6,2},{3,7},{7,3},{8,12},{12,8},{9,1... | collective-permute-start | bytes 2064392 | tf_op jit(solution)/shard_map/ppermute | solution.py:289
  22.1 46.3 %collective-permute-start.1 = (bf16[12,64,256]{2,1,0:T(8,128)(2,1)S(1)}, bf16[12,64,256]{2,1,0:T(8,128)(2,1)}, u32[]{:S(2)}, u32[]{:S(2)}) collective-permute-start(bf16[12,64,256]{2,1,0:T(8,128)(2,1)S(1)} %copy-done), channel_id=1, source_target_pairs={{0,4},{4,0},{1,5},{5,1},{2,6},{6,2},{3,7},{7,3},{8,12},{12,8},{9,1... | collective-permute-start | bytes 1179656 | tf_op jit(solution)/shard_map/ppermute | solution.py:289
  24.6 43.8 %collective-permute-start = (s32[15,64]{1,0:T(8,128)S(1)}, s32[15,64]{1,0:T(8,128)S(1)}, u32[]{:S(2)}, u32[]{:S(2)}) collective-permute-start(s32[15,64]{1,0:T(8,128)S(1)} %fusion.refs_1_), channel_id=1, source_target_pairs={{0,4},{4,0},{1,5},{5,1},{2,6},{6,2},{3,7},{7,3},{8,12},{12,8},{9,1... | collective-permute-start | bytes 11528 | tf_op jit(solution)/shard_map/ppermute | solution.py:289

commit v4 on v3

--- a/solution.py
+++ b/solution.py
@@ -78,38 +78,64 @@
     )(in_hbm(send_list), in_hbm(p_vals))
 
 
-def prepare_kernel(links, comp, where_ref, tables_ref, p_ref, a_ref, spread_ref, mixed_ref, local_ref, start_ref, source_ref, stacked):
-    rows, size, _ = p_ref.shape
-    width = a_ref.shape[2]
+def index_kernel(links, comp, place_ref, tables_ref, mine_ref, other_ref):
+    rows = 3 * PICKS
+    size = tables_ref.shape[1]
     w = size // 2
-    slots = tables_ref.shape[1]
-    half = where_ref[0]
-    place = where_ref[1]
+    place = place_ref[0]
+    shift = comp.bit_length() - 1
     for b in range(links):
         for r in range(rows):
             e = tables_ref[b, r]
+            is_local = e < rows
             near = jnp.minimum(e, rows - 1)
-            far = jnp.clip(e - rows, 0, slots - 1)
-            arrived = rows + (2 * (far // comp) + place) * comp + far % comp
-            source_ref[b, r] = jnp.where(e < rows, near, arrived)
+            far = jnp.clip(e - rows, 0, size - 1)
+            slot = ((far >> shift) << (shift + 1)) + (place << shift) + (far & (comp - 1))
+            source = jnp.where(is_local, near, rows + slot)
+            mine_ref[b, PICKS * rows + r] = source
+            other_ref[b, PICKS * rows + r] = source
             for k in range(PICKS):
-                c = jnp.where(e < rows, tables_ref[links + k, near], tables_ref[links + PICKS + k, far])
-                spot = c // 4 * 4 + c % 2 * 2 + jnp.where(half == 0, c // 2 % 2, 1 - c // 2 % 2)
-                start_ref[b, rows * k + r] = spot * w
+                c = jnp.where(is_local, tables_ref[links + k, near], tables_ref[links + PICKS + k, far])
+                base = (c & 12) + ((c & 1) << 1)
+                upper = (c >> 1) & 1
+                mine_ref[b, rows * k + r] = w * (base + (upper ^ place))
+                other_ref[b, rows * k + r] = w * (base + (upper ^ place ^ 1))
+    for k in range(PICKS):
+        for r in range(rows):
+            mine_ref[k, size + r] = tables_ref[links + k, r]
+            other_ref[k, size + r] = tables_ref[links + k, r]
+
+
+def index(links, comp, place, tables):
+    assert comp & (comp - 1) == 0
+    shape = jax.ShapeDtypeStruct((links, 2 * tables.shape[1]), jnp.int32)
+    return pl.pallas_call(
+        lambda *refs: index_kernel(links, comp, *refs),
+        out_shape=[shape, shape],
+        in_specs=[SMEM, SMEM],
+        out_specs=[SMEM, SMEM],
+        name="index",
+    )(place, tables)
+
+
+def layout_kernel(half_ref, table_ref, p_ref, spread_ref, local_ref):
+    rows, size, _ = p_ref.shape
+    w = size // 2
+    half = half_ref[0]
+    spread_ref[...] = jnp.zeros_like(spread_ref)
     flat = p_ref[...].reshape(rows * size, PICKS * size)
     row = lax.broadcasted_iota(jnp.int32, (PICKS * size, PICKS * size), 0)
     col = lax.broadcasted_iota(jnp.int32, (PICKS * size, PICKS * size), 1)
-    turned = lax.dot_general(one_hot(row == col), flat, NT, preferred_element_type=jnp.float32).astype(jnp.bfloat16)
-    spread_ref[...] = jnp.zeros_like(spread_ref)
+    turned = lax.dot_general(one_hot(row == col), flat, NT, preferred_element_type=jnp.float32)
     for r in range(rows):
         for k in range(PICKS):
-            start = pl.multiple_of(tables_ref[links + k, r] * size, size)
+            start = pl.multiple_of(table_ref[k, size + r] * size, size)
             spread_ref[pl.ds(start, size), r * size : (r + 1) * size] = turned[
                 k * size : (k + 1) * size, r * size : (r + 1) * size
-            ]
+            ].astype(jnp.bfloat16)
     row = lax.broadcasted_iota(jnp.int32, (size, PICKS * size), 0)
     col = lax.broadcasted_iota(jnp.int32, (size, PICKS * size), 1)
-    block = 2 * (row // w) * size + half * w + row % w
+    block = 2 * size * jnp.where(row < w, 0, 1) + half * w + jnp.where(row < w, row, row - w)
     lane = lax.broadcasted_iota(jnp.int32, (size, 2 * size), 1)
     packed = [
         lax.dot_general(one_hot(col == block + l * size), flat, NT, preferred_element_type=jnp.float32) for l in range(2)
@@ -119,43 +145,55 @@
         high = packed[1][:, u * 2 * size : (u + 1) * 2 * size]
         local_ref[2 * u] = jnp.where(lane < size, low, pltpu.roll(high, size, 1)).astype(jnp.bfloat16)
         local_ref[2 * u + 1] = jnp.where(lane < size, pltpu.roll(low, size, 1), high).astype(jnp.bfloat16)
+
+
+def layout(half, table, p_vals):
+    rows, size, _ = p_vals.shape
+    return pl.pallas_call(
+        layout_kernel,
+        out_shape=[
+            pltpu.HBM((NC * size, rows * size), p_vals.dtype),
+            pltpu.HBM((rows, size, 2 * size), p_vals.dtype),
+        ],
+        in_specs=[SMEM, SMEM, VMEM],
+        out_specs=[VMEM, VMEM],
+        compiler_params=pltpu.CompilerParams(vmem_limit_bytes=12 * MIB),
+        name="layout",
+    )(half, table, p_vals)
+
+
+def regroup_kernel(a_ref, mixed_ref, stacked):
+    rows, size, width = a_ref.shape
+    links = width // size
+    row = lax.broadcasted_iota(jnp.int32, (width, width), 0)
+    col = lax.broadcasted_iota(jnp.int32, (width, width), 1)
+    pair = links * (row & (size - 1)) + row // size
     for r in range(rows):
         for a in range(links):
             stacked[a * size : (a + 1) * size, r * size : (r + 1) * size] = a_ref[r, :, a * size : (a + 1) * size]
-    row = lax.broadcasted_iota(jnp.int32, (width, width), 0)
-    col = lax.broadcasted_iota(jnp.int32, (width, width), 1)
-    pair = links * (row % size) + row // size
     moved = lax.dot_general(one_hot(col == pair), stacked[...], NN, preferred_element_type=jnp.float32).astype(jnp.bfloat16)
     for r in range(rows):
         part = moved[:, r * size : (r + 1) * size]
         mixed_ref[r] = jnp.concatenate([part, part], axis=1)
 
 
-def prepare(comp, where, tables, p_vals, a_vals):
-    rows, size, _ = p_vals.shape
-    width = a_vals.shape[2]
-    links = width // size
-    return pl.pallas_call(
-        lambda *refs: prepare_kernel(links, comp, *refs),
-        out_shape=[
-            pltpu.HBM((NC * size, rows * size), p_vals.dtype),
-            pltpu.HBM((rows, width, 2 * size), p_vals.dtype),
-            pltpu.HBM((rows, size, 2 * size), p_vals.dtype),
-            jax.ShapeDtypeStruct((links, PICKS * rows), jnp.int32),
-            jax.ShapeDtypeStruct((links, rows), jnp.int32),
-        ],
-        in_specs=[SMEM, SMEM, VMEM, VMEM],
-        out_specs=[VMEM, VMEM, VMEM, SMEM, SMEM],
+def regroup(a_vals):
+    rows, size, width = a_vals.shape
+    return pl.pallas_call(
+        regroup_kernel,
+        out_shape=pltpu.HBM((rows, width, 2 * size), a_vals.dtype),
+        in_specs=[VMEM],
+        out_specs=VMEM,
         scratch_shapes=[pltpu.VMEM((width, rows * size), jnp.bfloat16)],
-        compiler_params=pltpu.CompilerParams(vmem_limit_bytes=20 * MIB),
-        name="prepare",
-    )(where, tables, p_vals, a_vals)
+        compiler_params=pltpu.CompilerParams(vmem_limit_bytes=16 * MIB),
+        name="regroup",
+    )(a_vals)
 
 
 def product_kernel(*refs):
-    starts, sources, spreads_hbm, mixed_hbm, local_hbm = (refs[i : i + 2] for i in range(0, 10, 2))
-    ghost_ref, out_ref, spread_ref, mixed_ref, local_ref, placed, picked, terms, prod, sems = refs[10:20]
-    sums = refs[20:]
+    tables, spreads_hbm, mixed_hbm, local_hbm = (refs[i : i + 2] for i in range(0, 8, 2))
+    ghost_ref, out_ref, spread_ref, mixed_ref, local_ref, placed, picked, terms, prod, sems = refs[8:18]
+    sums = refs[18:]
     _, rows, width, double = mixed_ref.shape
     size = double // 2
     w = size // 2
@@ -171,22 +209,29 @@
         total[...] = jnp.zeros_like(total)
     row = lax.broadcasted_iota(jnp.int32, (width, width), 0)
     col = lax.broadcasted_iota(jnp.int32, (width, width), 1)
-    keep = one_hot(col // size == (links * (row % size) + row // size) // size)
-    for copy in copies[:4]:
-        copy.wait()
+    near_link = (links * (row & (size - 1)) + row // size) // size
+    keep = one_hot(col // size == near_link)
     for o in range(2):
+        copies[o].wait()
         for r in range(rows):
             q = o * rows + r
             for a in range(links):
-                e = sources[o][a, r]
-                near = local_ref[o, jnp.minimum(e, rows - 1)]
-                far = ghost_ref[jnp.clip(e - rows, 0, slots - 1)]
-                source = jnp.where(e < rows, near, far)
+                if a == 0:
+                    source = local_ref[o, r]
+                else:
+                    e = tables[o][a, PICKS * rows + r]
+                    near = local_ref[o, jnp.minimum(e, rows - 1)]
+                    far = ghost_ref[jnp.clip(e - rows, 0, slots - 1)]
+                    source = jnp.where(e < rows, near, far)
                 for k in range(PICKS):
                     h, l = divmod(k, 2)
                     picked[q, k * w : (k + 1) * w, a * size : (a + 1) * size] = source[
                         h * w : (h + 1) * w, l * size : (l + 1) * size
                     ]
+    for o in range(2):
+        copies[2 + o].wait()
+        for r in range(rows):
+            q = o * rows + r
             twice = mixed_ref[o, r]
             for t in range(0, width, double):
                 stop = min(t + double, width)
@@ -197,7 +242,7 @@
             for odd in range(2):
                 for u in range(rows):
                     o, r = divmod(2 * u + odd, rows)
-                    here = pl.ds(pl.multiple_of(starts[o][b, rows * k + r], w), w)
+                    here = pl.ds(pl.multiple_of(tables[o][b, rows * k + r], w), w)
                     lanes = slice(odd * size, (odd + 1) * size)
                     sums[u][here, lanes] = (
                         sums[u][here, lanes] + terms[2 * u + odd, k * w : (k + 1) * w, b * size : (b + 1) * size]
@@ -214,19 +259,17 @@
 
 
 def product(mine, other, ghosts):
-    spread, mixed, local, _, _ = mine
+    _, spread, mixed, local = mine
     rows, width, double = mixed.shape
     size = double // 2
     wide = (NC + EXT) * (size // 2)
-    operands = []
-    for n in (3, 4):
-        operands += [mine[n], other[n]]
-    for n in (0, 1, 2):
+    operands = [mine[0], other[0]]
+    for n in (1, 2, 3):
         operands += [in_hbm(mine[n]), in_hbm(other[n])]
     return pl.pallas_call(
         product_kernel,
         out_shape=jax.ShapeDtypeStruct((NC * size, wide), jnp.bfloat16),
-        in_specs=[SMEM] * 4 + [HBM] * 6 + [VMEM],
+        in_specs=[SMEM] * 2 + [HBM] * 6 + [VMEM],
         out_specs=VMEM,
         scratch_shapes=[
             pltpu.VMEM((2, *spread.shape), jnp.bfloat16),
@@ -282,14 +325,19 @@
     outgoing = pack(send_list, p_vals, comp)
     outgoing = outgoing.reshape(-1, *outgoing.shape[3:])
     arrived = lax.all_to_all(outgoing, ("fine", "inner", "comp"), split_axis=0, concat_axis=0, tiled=True)
-    half = lax.axis_index("inner")
+    place = lax.axis_index("inner").reshape(1)
     columns = [jnp.pad(table.T, ((0, 0), (0, slots - table.shape[0]))) for table in (a_cols, p_cols, gp_cols)]
-    tables = jnp.concatenate(columns, axis=0)
     swap = ((0, 1), (1, 0))
-    a_other, p_other, tables_other = (lax.ppermute(array, "inner", swap) for array in (a_vals, p_vals, tables))
-    mine = prepare(comp, jnp.stack([half, half]), tables, p_vals, a_vals)
-    other = prepare(comp, jnp.stack([half, 1 - half]), tables_other, p_other, a_other)
-    partial = product(mine, other, arrived)
+    a_other = lax.ppermute(a_vals, "inner", swap)
+    table, table_sent = index(a_cols.shape[1], comp, place, jnp.concatenate(columns, axis=0))
+    table_other = lax.ppermute(table_sent, "inner", swap)
+    p_other = lax.ppermute(p_vals, "inner", swap)
+    spread, local = layout(place, table, p_vals)
+    mixed = regroup(a_vals)
+    mixed_other = regroup(a_other)
+    mixed_other, table_other, p_other = lax.optimization_barrier((mixed_other, table_other, p_other))
+    spread_other, local_other = layout(place, table_other, p_other)
+    partial = product((table, spread, mixed, local), (table_other, spread_other, mixed_other, local_other), arrived)
     moved = lax.all_to_all(partial, ("outer", "inner"), split_axis=0, concat_axis=0, tiled=True)
     owned = total(moved.reshape(NC, size, -1))
     return owned.reshape((1, owned.shape[0], 1, owned.shape[2]))

time: 113 us -> 106 us (0.938)
  Pallas kernels: 31.5 us -> 27.4 us
  waiting for transfers between devices: 31.9 us -> 28 us
    ppermute x3, waiting for transfers between devices: 31.9 us -> 28 us  [the longest x1 23.3 us: on_device(): a_other = lax.ppermute(a_vals, 'inner', swap)]
    pallas_call x2 -> x5, Pallas kernels: 17.2 us -> 14 us  [the longest x2 5.35 us: regroup(): pl.pallas_call(regroup_kernel, out_shape=pltpu.HBM((rows, width, 2 * size...]
  transfers between devices with their start and end apart: 4 -> 4, of which waited for: 1 -> 2; matrix products, arithmetic and copies ran while one was open for 0% -> 1% of each run, Pallas kernels for 15% -> 13%
where the time goes in v4:
time: 106 us; the launch traced here: 105 us
  waiting for transfers between devices  28 us (26%)
  Pallas kernels  27.4 us (26%)
  starting transfers between devices  25.1 us (24%)
  blocking collectives  23.3 us (22%)
    all_to_all x1, blocking collectives, on_device(): lax.all_to_all(partial, ('outer', 'inner'), split_axis=0, concat_axis=0,...  23.3 us
    ppermute x1, waiting for transfers between devices, on_device(): a_other = lax.ppermute(a_vals, 'inner', swap)  23.3 us
    all_to_all x1, starting transfers between devices, on_device(): lax.all_to_all(outgoing, ('fine', 'inner', 'comp'), split_axis=0, concat_...  15.8 us
    pallas_call x1, Pallas kernels, product(): pl.pallas_call(product_kernel, out_shape=jax.ShapeDtypeStruct((NC * size,...  9.67 us
    pallas_call x2, Pallas kernels, regroup(): pl.pallas_call(regroup_kernel, out_shape=pltpu.HBM((rows, width, 2 * size...  5.35 us
    ppermute x1, waiting for transfers between devices, on_device(): table_other = lax.ppermute(table_sent, 'inner', swap)  4.74 us
    pallas_call x2, Pallas kernels, layout(): pl.pallas_call(layout_kernel, out_shape=[pltpu.HBM((NC * size, rows * siz...  4.38 us
    pallas_call x1, Pallas kernels, index(): pl.pallas_call(lambda *refs: index_kernel(links, comp, *refs), out_shape=...  4.27 us
  transfers between devices with their start and end apart: 4, of which 2 were waited for; matrix products, arithmetic and copies ran while one was open for 1% of the time, Pallas kernels for 13%

profile of v4, /device:TPU:6, one launch (start us, length us, event | category | flops | bytes accessed | tf_op | source)
XLA Modules:
  0.0 104.7 jit_solution(12595879031626709394)
XLA Ops:
  0.0 2.8 %pack.1 = bf16[16,2,4,64,128]{4,3,2,1,0:T(8,128)(2,1)} custom-call(s32[64]{0:T(128)} %send_hbm.1, bf16[12,64,256]{2,1,0:T(8,128)(2,1)} %p_hbm.1), custom_call_target="tpu_custom_call" | custom-call | tf_op jit(solution)/shard_map/pack/pallas_call | solution.py:65
  2.8 0.0 copy-start.1
  2.8 0.0 copy-start
  2.9 0.0 copy-start.3
  2.9 0.0 copy-start.4
  2.9 0.0 copy-start.5
  2.9 15.8 %all-to-all-start = ((bf16[128,64,128]{2,1,0:T(8,128)(2,1)}), bf16[128,64,128]{2,1,0:T(8,128)(2,1)S(1)}, u32[]{:S(2)}, u32[]{:S(2)}) async-start(bf16[128,64,128]{2,1,0:T(8,128)(2,1)} %bitcast.8), calls=%async_computation | async-start | bytes 4194304 | tf_op jit(solution)/shard_map/all_to_all | solution.py:327
  18.7 3.4 %collective-permute-start = (bf16[12,64,448]{2,1,0:T(8,128)(2,1)S(1)}, bf16[12,64,448]{2,1,0:T(8,128)(2,1)}, u32[]{:S(2)}, u32[]{:S(2)}) collective-permute-start(bf16[12,64,448]{2,1,0:T(8,128)(2,1)S(1)} %copy-done.1), channel_id=1, source_target_pairs={{0,4},{4,0},{1,5},{5,1},{2,6},{6,2},{3,7},{7,3},{8,12},{12,8},{9,1... | collective-permute-start | bytes 2064392 | tf_op jit(solution)/shard_map/ppermute | solution.py:331
  22.0 0.0 copy-done
  22.1 2.5 %collective-permute-start.2 = (bf16[12,64,256]{2,1,0:T(8,128)(2,1)S(1)}, bf16[12,64,256]{2,1,0:T(8,128)(2,1)}, u32[]{:S(2)}, u32[]{:S(2)}) collective-permute-start(bf16[12,64,256]{2,1,0:T(8,128)(2,1)S(1)} %copy-done), channel_id=1, source_target_pairs={{0,4},{4,0},{1,5},{5,1},{2,6},{6,2},{3,7},{7,3},{8,12},{12,8},{9,1... | collective-permute-start | bytes 1179656 | tf_op jit(solution)/shard_map/ppermute | solution.py:334
  24.6 0.6 fusion.refs_1_
  25.2 4.3 %index.1 = (s32[7,128]{1,0:T(8,128)}, s32[7,128]{1,0:T(8,128)}) custom-call(s32[1]{0:T(128)} %bitcast.refs_0_.half_ref, s32[15,64]{1,0:T(8,128)} %fusion.refs_1_), custom_call_target="tpu_custom_call" | custom-call | tf_op jit(solution)/shard_map/index/pallas_call | solution.py:112
  29.5 3.6 %collective-permute-start.1 = (s32[7,128]{1,0:T(8,128)}, s32[7,128]{1,0:T(8,128)S(1)}, u32[]{:S(2)}, u32[]{:S(2)}) collective-permute-start(s32[7,128]{1,0:T(8,128)} %get-tuple-element.15), channel_id=1, source_target_pairs={{0,4},{4,0},{1,5},{5,1},{2,6},{6,2},{3,7},{7,3},{8,12},{12,8},{9,1... | collective-permute-start | bytes 10760 | tf_op jit(solution)/shard_map/ppermute | solution.py:333
  33.0 2.1 %regroup.3.refs_4_ = bf16[12,448,128]{2,1,0:T(8,128)(2,1)} custom-call(bf16[12,64,448]{2,1,0:T(8,128)(2,1)S(1)} %copy-done.1), custom_call_target="tpu_custom_call" | custom-call | tf_op jit(solution)/shard_map/regroup/pallas_call | solution.py:182
  35.1 2.0 %layout.2 = (bf16[512,768]{1,0:T(8,128)(2,1)}, bf16[12,64,128]{2,1,0:T(8,128)(2,1)}) custom-call(s32[1]{0:T(128)} %bitcast.refs_0_.half_ref, s32[7,128]{1,0:T(8,128)S(1)} %copy-done.2, bf16[12,64,256]{2,1,0:T(8,128)(2,1)S(1)} %copy-done), custom_call_target="tpu_custom_call" | custom-call | tf_op jit(solution)/shard_map/layout/pallas_call | solution.py:152
  37.1 23.3 %collective-permute-done.a_ref = bf16[12,64,448]{2,1,0:T(8,128)(2,1)} collective-permute-done((bf16[12,64,448]{2,1,0:T(8,128)(2,1)S(1)}, bf16[12,64,448]{2,1,0:T(8,128)(2,1)}, u32[]{:S(2)}, u32[]{:S(2)}) %collective-permute-start) | collective-permute-done | bytes 688160 | tf_op jit(solution)/shard_map/ppermute | solution.py:331
  60.4 3.3 %regroup.2.refs_5_ = bf16[12,448,128]{2,1,0:T(8,128)(2,1)} custom-call(bf16[12,64,448]{2,1,0:T(8,128)(2,1)} %collective-permute-done.a_ref), custom_call_target="tpu_custom_call" | custom-call | tf_op jit(solution)/shard_map/regroup/pallas_call | solution.py:182
  63.6 4.7 %collective-permute-done.1.table_ref.refs_1_ = s32[7,128]{1,0:T(8,128)S(1)} collective-permute-done((s32[7,128]{1,0:T(8,128)}, s32[7,128]{1,0:T(8,128)S(1)}, u32[]{:S(2)}, u32[]{:S(2)}) %collective-permute-start.1) | collective-permute-done | bytes 3616 | tf_op jit(solution)/shard_map/ppermute | solution.py:333
  68.4 0.0 collective-permute-done.2.p_ref
  68.4 2.4 %layout.3 = (bf16[512,768]{1,0:T(8,128)(2,1)}, bf16[12,64,128]{2,1,0:T(8,128)(2,1)}) custom-call(s32[1]{0:T(128)} %bitcast.refs_0_.half_ref, s32[7,128]{1,0:T(8,128)S(1)} %collective-permute-done.1.table_ref.refs_1_, bf16[12,64,256]{2,1,0:T(8,128)(2,1)} %collective-permute-done.2.p_ref), custom_call_target="tpu_custom_call" | custom-call | tf_op jit(solution)/shard_map/layout/pallas_call | solution.py:152
  70.8 0.0 all-to-all-done.refs_8_
  70.8 9.7 %product.1 = bf16[512,512]{1,0:T(8,128)(2,1)S(1)} custom-call(s32[7,128]{1,0:T(8,128)S(1)} %copy-done.2, s32[7,128]{1,0:T(8,128)S(1)} %collective-permute-done.1.table_ref.refs_1_, bf16[512,768]{1,0:T(8,128)(2,1)} %get-tuple-element.17.refs_2_, bf16[512,768]{1,0:T(8,128)(2,1)} %get-tuple-element.19.refs_3_, bf16[12,448,128]{2,1,0:T(8,128)(2,1)} %regroup.3.refs_4_, ...), custom_call_target="tpu_custom_call" | custom-call | tf_op jit(solution)/shard_map/product/pallas_call | solution.py:269
  80.5 23.3 %all_to_all.14.part_ref = bf16[8,64,512]{2,1,0:T(8,128)(2,1)S(1)} all-to-all(bf16[8,64,512]{2,1,0:T(8,128)(2,1)S(1)} %bitcast.7), channel_id=1, replica_groups=mesh['fine'=16,'outer'=4,'inner'=2,'comp'=4] {'outer','inner'}, dimensions={0} | all-to-all | bytes 1048576 | tf_op jit(solution)/shard_map/all_to_all | solution.py:341
  103.8 0.9 total.1
  (6 shorter events, 0.0 us)
Async XLA Ops:
  2.8 15.8 %copy-start.1 = (bf16[12,64,448]{2,1,0:T(8,128)(2,1)S(1)}, bf16[12,64,448]{2,1,0:T(8,128)(2,1)}, u32[]{:S(2)}) copy-start(bf16[12,64,448]{2,1,0:T(8,128)(2,1)} %a_ref.1) | copy-start | bytes 2064388
  2.8 19.2 %copy-start = (bf16[12,64,256]{2,1,0:T(8,128)(2,1)S(1)}, bf16[12,64,256]{2,1,0:T(8,128)(2,1)}, u32[]{:S(2)}) copy-start(bf16[12,64,256]{2,1,0:T(8,128)(2,1)} %p_hbm.1) | copy-start | bytes 1179652
  2.9 21.7 %copy-start.3 = (s32[12,7]{0,1:T(8,128)S(1)}, s32[12,7]{0,1:T(8,128)}, u32[]{:S(2)}) copy-start(s32[12,7]{0,1:T(8,128)} %param.7) | copy-start | bytes 1012
  2.9 21.7 %copy-start.4 = (s32[12,4]{0,1:T(4,128)S(1)}, s32[12,4]{0,1:T(4,128)}, u32[]{:S(2)}) copy-start(s32[12,4]{0,1:T(4,128)} %param.9) | copy-start | bytes 580
  2.9 21.7 %copy-start.5 = (s32[64,4]{0,1:T(4,128)S(1)}, s32[64,4]{0,1:T(4,128)}, u32[]{:S(2)}) copy-start(s32[64,4]{0,1:T(4,128)} %param.10) | copy-start | bytes 3076
  2.9 67.9 %all-to-all-start = ((bf16[128,64,128]{2,1,0:T(8,128)(2,1)}), bf16[128,64,128]{2,1,0:T(8,128)(2,1)S(1)}, u32[]{:S(2)}, u32[]{:S(2)}) async-start(bf16[128,64,128]{2,1,0:T(8,128)(2,1)} %bitcast.8), calls=%async_computation | async-start | bytes 4194304 | tf_op jit(solution)/shard_map/all_to_all | solution.py:327
  18.7 41.7 %collective-permute-start = (bf16[12,64,448]{2,1,0:T(8,128)(2,1)S(1)}, bf16[12,64,448]{2,1,0:T(8,128)(2,1)}, u32[]{:S(2)}, u32[]{:S(2)}) collective-permute-start(bf16[12,64,448]{2,1,0:T(8,128)(2,1)S(1)} %copy-done.1), channel_id=1, source_target_pairs={{0,4},{4,0},{1,5},{5,1},{2,6},{6,2},{3,7},{7,3},{8,12},{12,8},{9,1... | collective-permute-start | bytes 2064392 | tf_op jit(solution)/shard_map/ppermute | solution.py:331
  22.1 46.3 %collective-permute-start.2 = (bf16[12,64,256]{2,1,0:T(8,128)(2,1)S(1)}, bf16[12,64,256]{2,1,0:T(8,128)(2,1)}, u32[]{:S(2)}, u32[]{:S(2)}) collective-permute-start(bf16[12,64,256]{2,1,0:T(8,128)(2,1)S(1)} %copy-done), channel_id=1, source_target_pairs={{0,4},{4,0},{1,5},{5,1},{2,6},{6,2},{3,7},{7,3},{8,12},{12,8},{9,1... | collective-permute-start | bytes 1179656 | tf_op jit(solution)/shard_map/ppermute | solution.py:334
  29.5 5.7 %copy-start.2 = (s32[7,128]{1,0:T(8,128)S(1)}, s32[7,128]{1,0:T(8,128)}, u32[]{:S(2)}) copy-start(s32[7,128]{1,0:T(8,128)} %get-tuple-element.14.table_ref.refs_0_) | copy-start | bytes 10756
  29.5 38.9 %collective-permute-start.1 = (s32[7,128]{1,0:T(8,128)}, s32[7,128]{1,0:T(8,128)S(1)}, u32[]{:S(2)}, u32[]{:S(2)}) collective-permute-start(s32[7,128]{1,0:T(8,128)} %get-tuple-element.15), channel_id=1, source_target_pairs={{0,4},{4,0},{1,5},{5,1},{2,6},{6,2},{3,7},{7,3},{8,12},{12,8},{9,1... | collective-permute-start | bytes 10760 | tf_op jit(solution)/shard_map/ppermute | solution.py:333

commit v5 on v4

--- a/solution.py
+++ b/solution.py
@@ -118,11 +118,10 @@
     )(place, tables)
 
 
-def layout_kernel(half_ref, table_ref, p_ref, spread_ref, local_ref):
+def lay_out(half, table_ref, p_ref, spread_ref, local_ref):
     rows, size, _ = p_ref.shape
     w = size // 2
-    half = half_ref[0]
-    spread_ref[...] = jnp.zeros_like(spread_ref)
+    spread_ref[...] = jnp.zeros(spread_ref.shape, spread_ref.dtype)
     flat = p_ref[...].reshape(rows * size, PICKS * size)
     row = lax.broadcasted_iota(jnp.int32, (PICKS * size, PICKS * size), 0)
     col = lax.broadcasted_iota(jnp.int32, (PICKS * size, PICKS * size), 1)
@@ -147,6 +146,10 @@
         local_ref[2 * u + 1] = jnp.where(lane < size, pltpu.roll(low, size, 1), high).astype(jnp.bfloat16)
 
 
+def layout_kernel(half_ref, table_ref, p_ref, spread_ref, local_ref):
+    lay_out(half_ref[0], table_ref, p_ref, spread_ref, local_ref)
+
+
 def layout(half, table, p_vals):
     rows, size, _ = p_vals.shape
     return pl.pallas_call(
@@ -172,16 +175,20 @@
         for a in range(links):
             stacked[a * size : (a + 1) * size, r * size : (r + 1) * size] = a_ref[r, :, a * size : (a + 1) * size]
     moved = lax.dot_general(one_hot(col == pair), stacked[...], NN, preferred_element_type=jnp.float32).astype(jnp.bfloat16)
-    for r in range(rows):
-        part = moved[:, r * size : (r + 1) * size]
-        mixed_ref[r] = jnp.concatenate([part, part], axis=1)
+    row = lax.broadcasted_iota(jnp.int32, (4 * size, 4 * size), 0)
+    col = lax.broadcasted_iota(jnp.int32, (4 * size, 4 * size), 1)
+    eye = one_hot(row == col)
+    for r in range(0, rows, 4):
+        turned = lax.dot_general(eye, moved[:, r * size : (r + 4) * size], NT, preferred_element_type=jnp.float32)
+        for u in range(4):
+            mixed_ref[r + u] = turned[u * size : (u + 1) * size].astype(jnp.bfloat16)
 
 
 def regroup(a_vals):
     rows, size, width = a_vals.shape
     return pl.pallas_call(
         regroup_kernel,
-        out_shape=pltpu.HBM((rows, width, 2 * size), a_vals.dtype),
+        out_shape=pltpu.HBM((rows, size, width), a_vals.dtype),
         in_specs=[VMEM],
         out_specs=VMEM,
         scratch_shapes=[pltpu.VMEM((width, rows * size), jnp.bfloat16)],
@@ -191,28 +198,38 @@
 
 
 def product_kernel(*refs):
-    tables, spreads_hbm, mixed_hbm, local_hbm = (refs[i : i + 2] for i in range(0, 8, 2))
-    ghost_ref, out_ref, spread_ref, mixed_ref, local_ref, placed, picked, terms, prod, sems = refs[8:18]
-    sums = refs[18:]
-    _, rows, width, double = mixed_ref.shape
-    size = double // 2
+    half_ref, *tables, p_hbm, spread_hbm, local_hbm = refs[:6]
+    mixed_hbm = refs[6:8]
+    ghost_ref, out_ref, p_ref, spread_ref, mixed_ref, local_ref, placed, picked, terms, prod, sems = refs[8:19]
+    sums = refs[19:]
+    _, rows, size, width = mixed_ref.shape
+    double = 2 * size
     w = size // 2
     links = width // size
     slots = ghost_ref.shape[0]
-    copies = []
-    for n, (here, there) in enumerate(((local_hbm, local_ref), (mixed_hbm, mixed_ref), (spreads_hbm, spread_ref))):
-        for o in range(2):
-            copies.append(pltpu.make_async_copy(here[o], there.at[o], sems.at[2 * n + o]))
+    copies = [
+        pltpu.make_async_copy(here, there, sems.at[n])
+        for n, (here, there) in enumerate(
+            (
+                (p_hbm, p_ref),
+                (local_hbm, local_ref.at[0]),
+                (mixed_hbm[0], mixed_ref.at[0]),
+                (mixed_hbm[1], mixed_ref.at[1]),
+                (spread_hbm, spread_ref.at[0]),
+            )
+        )
+    ]
     for copy in copies:
         copy.start()
     for total in sums:
         total[...] = jnp.zeros_like(total)
-    row = lax.broadcasted_iota(jnp.int32, (width, width), 0)
-    col = lax.broadcasted_iota(jnp.int32, (width, width), 1)
-    near_link = (links * (row & (size - 1)) + row // size) // size
-    keep = one_hot(col // size == near_link)
+    row = lax.broadcasted_iota(jnp.int32, (links + 1, width), 0)
+    col = lax.broadcasted_iota(jnp.int32, (links + 1, width), 1)
+    keep = one_hot(row == (links * (col & (size - 1)) + col // size) // size)
+    copies[0].wait()
+    lay_out(half_ref[0], tables[1], p_ref, spread_ref.at[1], local_ref.at[1])
+    copies[1].wait()
     for o in range(2):
-        copies[o].wait()
         for r in range(rows):
             q = o * rows + r
             for a in range(links):
@@ -228,29 +245,34 @@
                     picked[q, k * w : (k + 1) * w, a * size : (a + 1) * size] = source[
                         h * w : (h + 1) * w, l * size : (l + 1) * size
                     ]
-    for o in range(2):
-        copies[2 + o].wait()
-        for r in range(rows):
-            q = o * rows + r
-            twice = mixed_ref[o, r]
-            for t in range(0, width, double):
-                stop = min(t + double, width)
-                placed[q, :, t:stop] = twice[:, : stop - t] * keep[:, t:stop]
-            terms[q] = lax.dot_general(picked[q], placed[q], NT, preferred_element_type=jnp.float32)
-    for b in range(links):
-        for k in range(PICKS):
-            for odd in range(2):
-                for u in range(rows):
-                    o, r = divmod(2 * u + odd, rows)
-                    here = pl.ds(pl.multiple_of(tables[o][b, rows * k + r], w), w)
-                    lanes = slice(odd * size, (odd + 1) * size)
-                    sums[u][here, lanes] = (
-                        sums[u][here, lanes] + terms[2 * u + odd, k * w : (k + 1) * w, b * size : (b + 1) * size]
-                    )
+    def expand(q):
+        o, r = divmod(q, rows)
+        if r == 0:
+            copies[2 + o].wait()
+        part = mixed_ref[o, r]
+        for a in range(links):
+            placed[q % 4, a * size : (a + 1) * size, :] = part * keep[a : a + 1, :]
+
+    expand(0)
+    for q in range(2 * rows):
+        if q + 1 < 2 * rows:
+            expand(q + 1)
+        terms[q] = lax.dot_general(picked[q], placed[q % 4], NN, preferred_element_type=jnp.float32)
+
+        if q % 4 == 3:
+            for b in range(links):
+                for k in range(PICKS):
+                    for odd in range(2):
+                        for u in (q // 2 - 1, q // 2):
+                            o, r = divmod(2 * u + odd, rows)
+                            here = pl.ds(pl.multiple_of(tables[o][b, rows * k + r], w), w)
+                            lanes = slice(odd * size, (odd + 1) * size)
+                            sums[u][here, lanes] = (
+                                sums[u][here, lanes] + terms[2 * u + odd, k * w : (k + 1) * w, b * size : (b + 1) * size]
+                            )
     for u in range(rows):
         prod[:, u * double : (u + 1) * double] = sums[u][...].astype(jnp.bfloat16)
-    for copy in copies[4:]:
-        copy.wait()
+    copies[4].wait()
     whole = rows * size
     out_ref[...] = (
         lax.dot_general(spread_ref[0], prod[:, :whole], NT, preferred_element_type=jnp.float32)
@@ -258,33 +280,30 @@
     ).astype(jnp.bfloat16)
 
 
-def product(mine, other, ghosts):
-    _, spread, mixed, local = mine
-    rows, width, double = mixed.shape
-    size = double // 2
+def product(half, tables, p_other, spread, local, mixed, ghosts):
+    rows, size, width = mixed[0].shape
     wide = (NC + EXT) * (size // 2)
-    operands = [mine[0], other[0]]
-    for n in (1, 2, 3):
-        operands += [in_hbm(mine[n]), in_hbm(other[n])]
+    operands = [in_hbm(array) for array in (p_other, spread, local, *mixed)]
     return pl.pallas_call(
         product_kernel,
         out_shape=jax.ShapeDtypeStruct((NC * size, wide), jnp.bfloat16),
-        in_specs=[SMEM] * 2 + [HBM] * 6 + [VMEM],
+        in_specs=[SMEM] * 3 + [HBM] * 5 + [VMEM],
         out_specs=VMEM,
         scratch_shapes=[
+            pltpu.VMEM(p_other.shape, jnp.bfloat16),
             pltpu.VMEM((2, *spread.shape), jnp.bfloat16),
-            pltpu.VMEM((2, *mixed.shape), jnp.bfloat16),
+            pltpu.VMEM((2, *mixed[0].shape), jnp.bfloat16),
             pltpu.VMEM((2, *local.shape), jnp.bfloat16),
-            pltpu.VMEM((2 * rows, width, width), jnp.bfloat16),
+            pltpu.VMEM((4, width, width), jnp.bfloat16),
             pltpu.VMEM((2 * rows, 2 * size, width), jnp.bfloat16),
             pltpu.VMEM((2 * rows, 2 * size, width), jnp.float32),
             pltpu.VMEM((wide, 2 * rows * size), jnp.bfloat16),
-            pltpu.SemaphoreType.DMA((6,)),
+            pltpu.SemaphoreType.DMA((5,)),
         ]
-        + [pltpu.VMEM((wide, double), jnp.float32)] * rows,
-        compiler_params=pltpu.CompilerParams(vmem_limit_bytes=44 * MIB),
+        + [pltpu.VMEM((wide, 2 * size), jnp.float32)] * rows,
+        compiler_params=pltpu.CompilerParams(vmem_limit_bytes=40 * MIB),
         name="product",
-    )(*operands, ghosts)
+    )(half, *tables, *operands, ghosts)
 
 
 def total_kernel(part_ref, out_ref):
@@ -336,8 +355,7 @@
     mixed = regroup(a_vals)
     mixed_other = regroup(a_other)
     mixed_other, table_other, p_other = lax.optimization_barrier((mixed_other, table_other, p_other))
-    spread_other, local_other = layout(place, table_other, p_other)
-    partial = product((table, spread, mixed, local), (table_other, spread_other, mixed_other, local_other), arrived)
+    partial = product(place, (table, table_other), p_other, spread, local, (mixed, mixed_other), arrived)
     moved = lax.all_to_all(partial, ("outer", "inner"), split_axis=0, concat_axis=0, tiled=True)
     owned = total(moved.reshape(NC, size, -1))
     return owned.reshape((1, owned.shape[0], 1, owned.shape[2]))

time: 106 us -> 103 us (0.972)
  Pallas kernels: 27.4 us -> 23.4 us
    pallas_call x2 -> x1, Pallas kernels: 4.38 us -> 1.96 us  [layout(): pl.pallas_call(layout_kernel, out_shape=[pltpu.HBM((NC * size, rows * siz...]
    pallas_call x1, Pallas kernels: 9.67 us -> 8.36 us  [product(): pl.pallas_call(product_kernel, out_shape=jax.ShapeDtypeStruct((NC * size,...]
  transfers between devices with their start and end apart: 4 -> 4, of which waited for: 2 -> 3; matrix products, arithmetic and copies ran while one was open for 1% -> 1% of each run, Pallas kernels for 13% -> 11%
where the time goes in v5:
time: 103 us; the launch traced here: 101 us
  waiting for transfers between devices  28.6 us (28%)
  starting transfers between devices  25.1 us (24%)
  Pallas kernels  23.4 us (23%)
  blocking collectives  22.9 us (22%)
    all_to_all x1, blocking collectives, on_device(): lax.all_to_all(partial, ('outer', 'inner'), split_axis=0, concat_axis=0,...  22.9 us
    ppermute x1, waiting for transfers between devices, on_device(): a_other = lax.ppermute(a_vals, 'inner', swap)  22.7 us
    all_to_all x1, starting transfers between devices, on_device(): lax.all_to_all(outgoing, ('fine', 'inner', 'comp'), split_axis=0, concat_...  15.8 us
    pallas_call x1, Pallas kernels, product(): pl.pallas_call(product_kernel, out_shape=jax.ShapeDtypeStruct((NC * size,...  8.36 us
    pallas_call x2, Pallas kernels, regroup(): pl.pallas_call(regroup_kernel, out_shape=pltpu.HBM((rows, size, width), a...  5.03 us
    ppermute x1, waiting for transfers between devices, on_device(): table_other = lax.ppermute(table_sent, 'inner', swap)  4.92 us
    pallas_call x1, Pallas kernels, index(): pl.pallas_call(lambda *refs: index_kernel(links, comp, *refs), out_shape=...  4.27 us
    ppermute x1, starting transfers between devices, on_device(): table_other = lax.ppermute(table_sent, 'inner', swap)  3.55 us
  transfers between devices with their start and end apart: 4, of which 3 were waited for; matrix products, arithmetic and copies ran while one was open for 1% of the time, Pallas kernels for 11%

profile of v5, /device:TPU:6, one launch (start us, length us, event | category | flops | bytes accessed | tf_op | source)
XLA Modules:
  0.0 101.5 jit_solution(13340317025190697311)
XLA Ops:
  0.0 2.8 %pack.1 = bf16[16,2,4,64,128]{4,3,2,1,0:T(8,128)(2,1)} custom-call(s32[64]{0:T(128)} %send_hbm.1, bf16[12,64,256]{2,1,0:T(8,128)(2,1)} %p_hbm.1), custom_call_target="tpu_custom_call" | custom-call | tf_op jit(solution)/shard_map/pack/pallas_call | solution.py:65
  2.8 0.0 copy-start.1
  2.8 0.0 copy-start
  2.9 0.0 copy-start.4
  2.9 0.0 copy-start.5
  2.9 0.0 copy-start.6
  2.9 15.8 %all-to-all-start = ((bf16[128,64,128]{2,1,0:T(8,128)(2,1)}), bf16[128,64,128]{2,1,0:T(8,128)(2,1)S(1)}, u32[]{:S(2)}, u32[]{:S(2)}) async-start(bf16[128,64,128]{2,1,0:T(8,128)(2,1)} %bitcast.8), calls=%async_computation | async-start | bytes 4194304 | tf_op jit(solution)/shard_map/all_to_all | solution.py:346
  18.7 3.4 %collective-permute-start = (bf16[12,64,448]{2,1,0:T(8,128)(2,1)S(1)}, bf16[12,64,448]{2,1,0:T(8,128)(2,1)}, u32[]{:S(2)}, u32[]{:S(2)}) collective-permute-start(bf16[12,64,448]{2,1,0:T(8,128)(2,1)S(1)} %copy-done.1), channel_id=1, source_target_pairs={{0,4},{4,0},{1,5},{5,1},{2,6},{6,2},{3,7},{7,3},{8,12},{12,8},{9,1... | collective-permute-start | bytes 2064392 | tf_op jit(solution)/shard_map/ppermute | solution.py:350
  22.0 0.0 copy-done
  22.1 2.5 %collective-permute-start.2 = (bf16[12,64,256]{2,1,0:T(8,128)(2,1)S(1)}, bf16[12,64,256]{2,1,0:T(8,128)(2,1)}, u32[]{:S(2)}, u32[]{:S(2)}) collective-permute-start(bf16[12,64,256]{2,1,0:T(8,128)(2,1)S(1)} %copy-done), channel_id=1, source_target_pairs={{0,4},{4,0},{1,5},{5,1},{2,6},{6,2},{3,7},{7,3},{8,12},{12,8},{9,1... | collective-permute-start | bytes 1179656 | tf_op jit(solution)/shard_map/ppermute | solution.py:353
  24.6 0.6 fusion.refs_1_
  25.2 4.3 %index.1 = (s32[7,128]{1,0:T(8,128)}, s32[7,128]{1,0:T(8,128)}) custom-call(s32[1]{0:T(128)} %bitcast.refs_0_.half_ref, s32[15,64]{1,0:T(8,128)} %fusion.refs_1_), custom_call_target="tpu_custom_call" | custom-call | tf_op jit(solution)/shard_map/index/pallas_call | solution.py:112
  29.5 3.6 %collective-permute-start.1 = (s32[7,128]{1,0:T(8,128)}, s32[7,128]{1,0:T(8,128)S(1)}, u32[]{:S(2)}, u32[]{:S(2)}) collective-permute-start(s32[7,128]{1,0:T(8,128)} %get-tuple-element.13), channel_id=1, source_target_pairs={{0,4},{4,0},{1,5},{5,1},{2,6},{6,2},{3,7},{7,3},{8,12},{12,8},{9,1... | collective-permute-start | bytes 10760 | tf_op jit(solution)/shard_map/ppermute | solution.py:352
  33.0 2.0 %regroup.3.refs_6_ = bf16[12,64,448]{2,1,0:T(8,128)(2,1)} custom-call(bf16[12,64,448]{2,1,0:T(8,128)(2,1)S(1)} %copy-done.1), custom_call_target="tpu_custom_call" | custom-call | tf_op jit(solution)/shard_map/regroup/pallas_call | solution.py:189
  35.0 0.7 copy-done.2
  35.7 2.0 %layout.1 = (bf16[512,768]{1,0:T(8,128)(2,1)}, bf16[12,64,128]{2,1,0:T(8,128)(2,1)}) custom-call(s32[1]{0:T(128)} %bitcast.refs_0_.half_ref, s32[7,128]{1,0:T(8,128)S(1)} %copy-done.2, bf16[12,64,256]{2,1,0:T(8,128)(2,1)S(1)} %copy-done), custom_call_target="tpu_custom_call" | custom-call | tf_op jit(solution)/shard_map/layout/pallas_call | solution.py:155
  37.6 22.7 %collective-permute-done.a_ref = bf16[12,64,448]{2,1,0:T(8,128)(2,1)} collective-permute-done((bf16[12,64,448]{2,1,0:T(8,128)(2,1)S(1)}, bf16[12,64,448]{2,1,0:T(8,128)(2,1)}, u32[]{:S(2)}, u32[]{:S(2)}) %collective-permute-start) | collective-permute-done | bytes 688160 | tf_op jit(solution)/shard_map/ppermute | solution.py:350
  60.4 3.1 %regroup.2.refs_7_ = bf16[12,64,448]{2,1,0:T(8,128)(2,1)} custom-call(bf16[12,64,448]{2,1,0:T(8,128)(2,1)} %collective-permute-done.a_ref), custom_call_target="tpu_custom_call" | custom-call | tf_op jit(solution)/shard_map/regroup/pallas_call | solution.py:189
  63.4 4.9 %collective-permute-done.1.refs_2_ = s32[7,128]{1,0:T(8,128)S(1)} collective-permute-done((s32[7,128]{1,0:T(8,128)}, s32[7,128]{1,0:T(8,128)S(1)}, u32[]{:S(2)}, u32[]{:S(2)}) %collective-permute-start.1) | collective-permute-done | bytes 3616 | tf_op jit(solution)/shard_map/ppermute | solution.py:352
  68.4 0.0 collective-permute-done.2.refs_3_
  68.4 1.0 all-to-all-done.refs_8_
  69.3 8.4 %product.1 = bf16[512,512]{1,0:T(8,128)(2,1)S(1)} custom-call(s32[1]{0:T(128)} %bitcast.refs_0_.half_ref, s32[7,128]{1,0:T(8,128)S(1)} %copy-done.3, s32[7,128]{1,0:T(8,128)S(1)} %collective-permute-done.1.refs_2_, bf16[12,64,256]{2,1,0:T(8,128)(2,1)} %collective-permute-done.2.refs_3_, bf16[512,768]{1,0:T(8,128)(2,1)} %get-tuple-element.16.refs_4_, ...), custom_call_target="tpu_custom_call" | custom-call | tf_op jit(solution)/shard_map/product/pallas_call | solution.py:287
  77.7 22.9 %all_to_all.14.part_ref = bf16[8,64,512]{2,1,0:T(8,128)(2,1)S(1)} all-to-all(bf16[8,64,512]{2,1,0:T(8,128)(2,1)S(1)} %bitcast.7), channel_id=1, replica_groups=mesh['fine'=16,'outer'=4,'inner'=2,'comp'=4] {'outer','inner'}, dimensions={0} | all-to-all | bytes 1048576 | tf_op jit(solution)/shard_map/all_to_all | solution.py:359
  100.6 0.9 total.1
  (7 shorter events, 0.0 us)
Async XLA Ops:
  2.8 15.8 %copy-start.1 = (bf16[12,64,448]{2,1,0:T(8,128)(2,1)S(1)}, bf16[12,64,448]{2,1,0:T(8,128)(2,1)}, u32[]{:S(2)}) copy-start(bf16[12,64,448]{2,1,0:T(8,128)(2,1)} %a_ref.1) | copy-start | bytes 2064388
  2.8 19.2 %copy-start = (bf16[12,64,256]{2,1,0:T(8,128)(2,1)S(1)}, bf16[12,64,256]{2,1,0:T(8,128)(2,1)}, u32[]{:S(2)}) copy-start(bf16[12,64,256]{2,1,0:T(8,128)(2,1)} %p_hbm.1) | copy-start | bytes 1179652
  2.9 21.7 %copy-start.4 = (s32[12,7]{0,1:T(8,128)S(1)}, s32[12,7]{0,1:T(8,128)}, u32[]{:S(2)}) copy-start(s32[12,7]{0,1:T(8,128)} %param.7) | copy-start | bytes 1012
  2.9 21.7 %copy-start.5 = (s32[12,4]{0,1:T(4,128)S(1)}, s32[12,4]{0,1:T(4,128)}, u32[]{:S(2)}) copy-start(s32[12,4]{0,1:T(4,128)} %param.9) | copy-start | bytes 580
  2.9 21.7 %copy-start.6 = (s32[64,4]{0,1:T(4,128)S(1)}, s32[64,4]{0,1:T(4,128)}, u32[]{:S(2)}) copy-start(s32[64,4]{0,1:T(4,128)} %param.10) | copy-start | bytes 3076
  2.9 66.4 %all-to-all-start = ((bf16[128,64,128]{2,1,0:T(8,128)(2,1)}), bf16[128,64,128]{2,1,0:T(8,128)(2,1)S(1)}, u32[]{:S(2)}, u32[]{:S(2)}) async-start(bf16[128,64,128]{2,1,0:T(8,128)(2,1)} %bitcast.8), calls=%async_computation | async-start | bytes 4194304 | tf_op jit(solution)/shard_map/all_to_all | solution.py:346
  18.7 41.7 %collective-permute-start = (bf16[12,64,448]{2,1,0:T(8,128)(2,1)S(1)}, bf16[12,64,448]{2,1,0:T(8,128)(2,1)}, u32[]{:S(2)}, u32[]{:S(2)}) collective-permute-start(bf16[12,64,448]{2,1,0:T(8,128)(2,1)S(1)} %copy-done.1), channel_id=1, source_target_pairs={{0,4},{4,0},{1,5},{5,1},{2,6},{6,2},{3,7},{7,3},{8,12},{12,8},{9,1... | collective-permute-start | bytes 2064392 | tf_op jit(solution)/shard_map/ppermute | solution.py:350
  22.1 46.3 %collective-permute-start.2 = (bf16[12,64,256]{2,1,0:T(8,128)(2,1)S(1)}, bf16[12,64,256]{2,1,0:T(8,128)(2,1)}, u32[]{:S(2)}, u32[]{:S(2)}) collective-permute-start(bf16[12,64,256]{2,1,0:T(8,128)(2,1)S(1)} %copy-done), channel_id=1, source_target_pairs={{0,4},{4,0},{1,5},{5,1},{2,6},{6,2},{3,7},{7,3},{8,12},{12,8},{9,1... | collective-permute-start | bytes 1179656 | tf_op jit(solution)/shard_map/ppermute | solution.py:353
  29.5 39.9 %copy-start.3 = (s32[7,128]{1,0:T(8,128)S(1)}, s32[7,128]{1,0:T(8,128)}, u32[]{:S(2)}) copy-start(s32[7,128]{1,0:T(8,128)} %get-tuple-element.12.table_ref.refs_1_) | copy-start | bytes 10756
  29.5 38.9 %collective-permute-start.1 = (s32[7,128]{1,0:T(8,128)}, s32[7,128]{1,0:T(8,128)S(1)}, u32[]{:S(2)}, u32[]{:S(2)}) collective-permute-start(s32[7,128]{1,0:T(8,128)} %get-tuple-element.13), channel_id=1, source_target_pairs={{0,4},{4,0},{1,5},{5,1},{2,6},{6,2},{3,7},{7,3},{8,12},{12,8},{9,1... | collective-permute-start | bytes 10760 | tf_op jit(solution)/shard_map/ppermute | solution.py:352
  35.0 0.7 copy-start.2

commit v6 on v5

--- a/solution.py
+++ b/solution.py
@@ -229,22 +229,32 @@
     copies[0].wait()
     lay_out(half_ref[0], tables[1], p_ref, spread_ref.at[1], local_ref.at[1])
     copies[1].wait()
+    lane = lax.broadcasted_iota(jnp.int32, (size, double), 1)
+
+    def source(o, r, a):
+        if a == 0:
+            return local_ref[o, r]
+        e = tables[o][a, PICKS * rows + r]
+        near = local_ref[o, jnp.minimum(e, rows - 1)]
+        far = ghost_ref[jnp.clip(e - rows, 0, slots - 1)]
+        return jnp.where(e < rows, near, far)
+
     for o in range(2):
         for r in range(rows):
             q = o * rows + r
-            for a in range(links):
-                if a == 0:
-                    source = local_ref[o, r]
+            for a in range(0, links, 2):
+                low = source(o, r, a)
+                if a + 1 < links:
+                    high = source(o, r, a + 1)
+                    blocks = [
+                        jnp.where(lane < size, low, pltpu.roll(high, size, 1)),
+                        jnp.where(lane < size, pltpu.roll(low, size, 1), high),
+                    ]
                 else:
-                    e = tables[o][a, PICKS * rows + r]
-                    near = local_ref[o, jnp.minimum(e, rows - 1)]
-                    far = ghost_ref[jnp.clip(e - rows, 0, slots - 1)]
-                    source = jnp.where(e < rows, near, far)
+                    blocks = [low[:, :size], low[:, size:]]
                 for k in range(PICKS):
                     h, l = divmod(k, 2)
-                    picked[q, k * w : (k + 1) * w, a * size : (a + 1) * size] = source[
-                        h * w : (h + 1) * w, l * size : (l + 1) * size
-                    ]
+                    picked[q, k * w : (k + 1) * w, a * size : min(a + 2, links) * size] = blocks[l][h * w : (h + 1) * w]
     def expand(q):
         o, r = divmod(q, rows)
         if r == 0:
@@ -253,31 +263,42 @@
         for a in range(links):
             placed[q % 4, a * size : (a + 1) * size, :] = part * keep[a : a + 1, :]
 
+    def add(pairs):
+        for b in range(links):
+            for k in range(PICKS):
+                for odd in range(2):
+                    for u in pairs:
+                        o, r = divmod(2 * u + odd, rows)
+                        here = pl.ds(pl.multiple_of(tables[o][b, rows * k + r], w), w)
+                        lanes = slice(odd * size, (odd + 1) * size)
+                        sums[u][here, lanes] = (
+                            sums[u][here, lanes] + terms[2 * u + odd, k * w : (k + 1) * w, b * size : (b + 1) * size]
+                        )
+        for u in pairs:
+            prod[:, u * double : (u + 1) * double] = sums[u][...].astype(jnp.bfloat16)
+
+    whole = rows * size
+    first = []
+
+    def contract(o):
+        return lax.dot_general(
+            spread_ref[o], prod[:, o * whole : (o + 1) * whole], NT, preferred_element_type=jnp.float32
+        )
+
+    copies[4].wait()
     expand(0)
     for q in range(2 * rows):
         if q + 1 < 2 * rows:
             expand(q + 1)
         terms[q] = lax.dot_general(picked[q], placed[q % 4], NN, preferred_element_type=jnp.float32)
-
         if q % 4 == 3:
-            for b in range(links):
-                for k in range(PICKS):
-                    for odd in range(2):
-                        for u in (q // 2 - 1, q // 2):
-                            o, r = divmod(2 * u + odd, rows)
-                            here = pl.ds(pl.multiple_of(tables[o][b, rows * k + r], w), w)
-                            lanes = slice(odd * size, (odd + 1) * size)
-                            sums[u][here, lanes] = (
-                                sums[u][here, lanes] + terms[2 * u + odd, k * w : (k + 1) * w, b * size : (b + 1) * size]
-                            )
-    for u in range(rows):
-        prod[:, u * double : (u + 1) * double] = sums[u][...].astype(jnp.bfloat16)
-    copies[4].wait()
-    whole = rows * size
-    out_ref[...] = (
-        lax.dot_general(spread_ref[0], prod[:, :whole], NT, preferred_element_type=jnp.float32)
-        + lax.dot_general(spread_ref[1], prod[:, whole:], NT, preferred_element_type=jnp.float32)
-    ).astype(jnp.bfloat16)
+            u = q // 2 - 2
+            if u >= 1:
+                add((u - 1, u))
+            if u == rows // 2 - 1:
+                first.append(contract(0))
+    add((rows - 2, rows - 1))
+    out_ref[...] = (first[0] + contract(1)).astype(jnp.bfloat16)
 
 
 def product(half, tables, p_other, spread, local, mixed, ghosts):

time: 103 us -> 102 us (level)
  no operation moved by 1% of the time
where the time goes in v6:
time: 102 us; the launch traced here: 101 us
  waiting for transfers between devices  28.6 us (28%)
  starting transfers between devices  25.1 us (25%)
  blocking collectives  22.9 us (22%)
  Pallas kernels  22.5 us (22%)
    all_to_all x1, blocking collectives, on_device(): lax.all_to_all(partial, ('outer', 'inner'), split_axis=0, concat_axis=0,...  22.9 us
    ppermute x1, waiting for transfers between devices, on_device(): a_other = lax.ppermute(a_vals, 'inner', swap)  22.7 us
    all_to_all x1, starting transfers between devices, on_device(): lax.all_to_all(outgoing, ('fine', 'inner', 'comp'), split_axis=0, concat_...  15.8 us
    pallas_call x1, Pallas kernels, product(): pl.pallas_call(product_kernel, out_shape=jax.ShapeDtypeStruct((NC * size,...  7.49 us
    pallas_call x2, Pallas kernels, regroup(): pl.pallas_call(regroup_kernel, out_shape=pltpu.HBM((rows, size, width), a...  5.03 us
    ppermute x1, waiting for transfers between devices, on_device(): table_other = lax.ppermute(table_sent, 'inner', swap)  4.92 us
    pallas_call x1, Pallas kernels, index(): pl.pallas_call(lambda *refs: index_kernel(links, comp, *refs), out_shape=...  4.27 us
    ppermute x1, starting transfers between devices, on_device(): table_other = lax.ppermute(table_sent, 'inner', swap)  3.55 us
  transfers between devices with their start and end apart: 4, of which 3 were waited for; matrix products, arithmetic and copies ran while one was open for 1% of the time, Pallas kernels for 11%

profile of v6, /device:TPU:6, one launch (start us, length us, event | category | flops | bytes accessed | tf_op | source)
XLA Modules:
  0.0 100.6 jit_solution(171485362303185978)
XLA Ops:
  0.0 2.8 %pack.1 = bf16[16,2,4,64,128]{4,3,2,1,0:T(8,128)(2,1)} custom-call(s32[64]{0:T(128)} %send_hbm.1, bf16[12,64,256]{2,1,0:T(8,128)(2,1)} %p_hbm.1), custom_call_target="tpu_custom_call" | custom-call | tf_op jit(solution)/shard_map/pack/pallas_call | solution.py:65
  2.8 0.0 copy-start.1
  2.8 0.0 copy-start
  2.9 0.0 copy-start.4
  2.9 0.0 copy-start.5
  2.9 0.0 copy-start.6
  2.9 15.8 %all-to-all-start = ((bf16[128,64,128]{2,1,0:T(8,128)(2,1)}), bf16[128,64,128]{2,1,0:T(8,128)(2,1)S(1)}, u32[]{:S(2)}, u32[]{:S(2)}) async-start(bf16[128,64,128]{2,1,0:T(8,128)(2,1)} %bitcast.8), calls=%async_computation | async-start | bytes 4194304 | tf_op jit(solution)/shard_map/all_to_all | solution.py:367
  18.7 0.0 copy-done.1
  18.7 3.4 %collective-permute-start = (bf16[12,64,448]{2,1,0:T(8,128)(2,1)S(1)}, bf16[12,64,448]{2,1,0:T(8,128)(2,1)}, u32[]{:S(2)}, u32[]{:S(2)}) collective-permute-start(bf16[12,64,448]{2,1,0:T(8,128)(2,1)S(1)} %copy-done.1), channel_id=1, source_target_pairs={{0,4},{4,0},{1,5},{5,1},{2,6},{6,2},{3,7},{7,3},{8,12},{12,8},{9,1... | collective-permute-start | bytes 2064392 | tf_op jit(solution)/shard_map/ppermute | solution.py:371
  22.1 2.5 %collective-permute-start.2 = (bf16[12,64,256]{2,1,0:T(8,128)(2,1)S(1)}, bf16[12,64,256]{2,1,0:T(8,128)(2,1)}, u32[]{:S(2)}, u32[]{:S(2)}) collective-permute-start(bf16[12,64,256]{2,1,0:T(8,128)(2,1)S(1)} %copy-done), channel_id=1, source_target_pairs={{0,4},{4,0},{1,5},{5,1},{2,6},{6,2},{3,7},{7,3},{8,12},{12,8},{9,1... | collective-permute-start | bytes 1179656 | tf_op jit(solution)/shard_map/ppermute | solution.py:374
  24.6 0.6 fusion.refs_1_
  25.2 4.3 %index.1 = (s32[7,128]{1,0:T(8,128)}, s32[7,128]{1,0:T(8,128)}) custom-call(s32[1]{0:T(128)} %bitcast.refs_0_.half_ref, s32[15,64]{1,0:T(8,128)} %fusion.refs_1_), custom_call_target="tpu_custom_call" | custom-call | tf_op jit(solution)/shard_map/index/pallas_call | solution.py:112
  29.5 3.6 %collective-permute-start.1 = (s32[7,128]{1,0:T(8,128)}, s32[7,128]{1,0:T(8,128)S(1)}, u32[]{:S(2)}, u32[]{:S(2)}) collective-permute-start(s32[7,128]{1,0:T(8,128)} %get-tuple-element.13), channel_id=1, source_target_pairs={{0,4},{4,0},{1,5},{5,1},{2,6},{6,2},{3,7},{7,3},{8,12},{12,8},{9,1... | collective-permute-start | bytes 10760 | tf_op jit(solution)/shard_map/ppermute | solution.py:373
  33.0 2.0 %regroup.3.refs_6_ = bf16[12,64,448]{2,1,0:T(8,128)(2,1)} custom-call(bf16[12,64,448]{2,1,0:T(8,128)(2,1)S(1)} %copy-done.1), custom_call_target="tpu_custom_call" | custom-call | tf_op jit(solution)/shard_map/regroup/pallas_call | solution.py:189
  35.0 0.7 copy-done.2
  35.7 2.0 %layout.1 = (bf16[512,768]{1,0:T(8,128)(2,1)}, bf16[12,64,128]{2,1,0:T(8,128)(2,1)}) custom-call(s32[1]{0:T(128)} %bitcast.refs_0_.half_ref, s32[7,128]{1,0:T(8,128)S(1)} %copy-done.2, bf16[12,64,256]{2,1,0:T(8,128)(2,1)S(1)} %copy-done), custom_call_target="tpu_custom_call" | custom-call | tf_op jit(solution)/shard_map/layout/pallas_call | solution.py:155
  37.6 22.7 %collective-permute-done.a_ref = bf16[12,64,448]{2,1,0:T(8,128)(2,1)} collective-permute-done((bf16[12,64,448]{2,1,0:T(8,128)(2,1)S(1)}, bf16[12,64,448]{2,1,0:T(8,128)(2,1)}, u32[]{:S(2)}, u32[]{:S(2)}) %collective-permute-start) | collective-permute-done | bytes 688160 | tf_op jit(solution)/shard_map/ppermute | solution.py:371
  60.4 3.1 %regroup.2.refs_7_ = bf16[12,64,448]{2,1,0:T(8,128)(2,1)} custom-call(bf16[12,64,448]{2,1,0:T(8,128)(2,1)} %collective-permute-done.a_ref), custom_call_target="tpu_custom_call" | custom-call | tf_op jit(solution)/shard_map/regroup/pallas_call | solution.py:189
  63.4 4.9 %collective-permute-done.1.refs_2_ = s32[7,128]{1,0:T(8,128)S(1)} collective-permute-done((s32[7,128]{1,0:T(8,128)}, s32[7,128]{1,0:T(8,128)S(1)}, u32[]{:S(2)}, u32[]{:S(2)}) %collective-permute-start.1) | collective-permute-done | bytes 3616 | tf_op jit(solution)/shard_map/ppermute | solution.py:373
  68.4 0.0 collective-permute-done.2.refs_3_
  68.4 1.0 all-to-all-done.refs_8_
  69.3 7.5 %product.1 = bf16[512,512]{1,0:T(8,128)(2,1)S(1)} custom-call(s32[1]{0:T(128)} %bitcast.refs_0_.half_ref, s32[7,128]{1,0:T(8,128)S(1)} %copy-done.3, s32[7,128]{1,0:T(8,128)S(1)} %collective-permute-done.1.refs_2_, bf16[12,64,256]{2,1,0:T(8,128)(2,1)} %collective-permute-done.2.refs_3_, bf16[512,768]{1,0:T(8,128)(2,1)} %get-tuple-element.16.refs_4_, ...), custom_call_target="tpu_custom_call" | custom-call | tf_op jit(solution)/shard_map/product/pallas_call | solution.py:308
  76.8 22.9 %all_to_all.14.part_ref = bf16[8,64,512]{2,1,0:T(8,128)(2,1)S(1)} all-to-all(bf16[8,64,512]{2,1,0:T(8,128)(2,1)S(1)} %bitcast.7), channel_id=1, replica_groups=mesh['fine'=16,'outer'=4,'inner'=2,'comp'=4] {'outer','inner'}, dimensions={0} | all-to-all | bytes 1048576 | tf_op jit(solution)/shard_map/all_to_all | solution.py:380
  99.7 0.9 total.1
  (7 shorter events, 0.0 us)
Async XLA Ops:
  2.8 15.8 %copy-start.1 = (bf16[12,64,448]{2,1,0:T(8,128)(2,1)S(1)}, bf16[12,64,448]{2,1,0:T(8,128)(2,1)}, u32[]{:S(2)}) copy-start(bf16[12,64,448]{2,1,0:T(8,128)(2,1)} %a_ref.1) | copy-start | bytes 2064388
  2.8 19.2 %copy-start = (bf16[12,64,256]{2,1,0:T(8,128)(2,1)S(1)}, bf16[12,64,256]{2,1,0:T(8,128)(2,1)}, u32[]{:S(2)}) copy-start(bf16[12,64,256]{2,1,0:T(8,128)(2,1)} %p_hbm.1) | copy-start | bytes 1179652
  2.9 21.7 %copy-start.4 = (s32[12,7]{0,1:T(8,128)S(1)}, s32[12,7]{0,1:T(8,128)}, u32[]{:S(2)}) copy-start(s32[12,7]{0,1:T(8,128)} %param.7) | copy-start | bytes 1012
  2.9 21.7 %copy-start.5 = (s32[12,4]{0,1:T(4,128)S(1)}, s32[12,4]{0,1:T(4,128)}, u32[]{:S(2)}) copy-start(s32[12,4]{0,1:T(4,128)} %param.9) | copy-start | bytes 580
  2.9 21.7 %copy-start.6 = (s32[64,4]{0,1:T(4,128)S(1)}, s32[64,4]{0,1:T(4,128)}, u32[]{:S(2)}) copy-start(s32[64,4]{0,1:T(4,128)} %param.10) | copy-start | bytes 3076
  2.9 66.4 %all-to-all-start = ((bf16[128,64,128]{2,1,0:T(8,128)(2,1)}), bf16[128,64,128]{2,1,0:T(8,128)(2,1)S(1)}, u32[]{:S(2)}, u32[]{:S(2)}) async-start(bf16[128,64,128]{2,1,0:T(8,128)(2,1)} %bitcast.8), calls=%async_computation | async-start | bytes 4194304 | tf_op jit(solution)/shard_map/all_to_all | solution.py:367
  18.7 41.7 %collective-permute-start = (bf16[12,64,448]{2,1,0:T(8,128)(2,1)S(1)}, bf16[12,64,448]{2,1,0:T(8,128)(2,1)}, u32[]{:S(2)}, u32[]{:S(2)}) collective-permute-start(bf16[12,64,448]{2,1,0:T(8,128)(2,1)S(1)} %copy-done.1), channel_id=1, source_target_pairs={{0,4},{4,0},{1,5},{5,1},{2,6},{6,2},{3,7},{7,3},{8,12},{12,8},{9,1... | collective-permute-start | bytes 2064392 | tf_op jit(solution)/shard_map/ppermute | solution.py:371
  22.1 46.3 %collective-permute-start.2 = (bf16[12,64,256]{2,1,0:T(8,128)(2,1)S(1)}, bf16[12,64,256]{2,1,0:T(8,128)(2,1)}, u32[]{:S(2)}, u32[]{:S(2)}) collective-permute-start(bf16[12,64,256]{2,1,0:T(8,128)(2,1)S(1)} %copy-done), channel_id=1, source_target_pairs={{0,4},{4,0},{1,5},{5,1},{2,6},{6,2},{3,7},{7,3},{8,12},{12,8},{9,1... | collective-permute-start | bytes 1179656 | tf_op jit(solution)/shard_map/ppermute | solution.py:374
  29.5 39.9 %copy-start.3 = (s32[7,128]{1,0:T(8,128)S(1)}, s32[7,128]{1,0:T(8,128)}, u32[]{:S(2)}) copy-start(s32[7,128]{1,0:T(8,128)} %get-tuple-element.12.table_ref.refs_1_) | copy-start | bytes 10756
  29.5 38.9 %collective-permute-start.1 = (s32[7,128]{1,0:T(8,128)}, s32[7,128]{1,0:T(8,128)S(1)}, u32[]{:S(2)}, u32[]{:S(2)}) collective-permute-start(s32[7,128]{1,0:T(8,128)} %get-tuple-element.13), channel_id=1, source_target_pairs={{0,4},{4,0},{1,5},{5,1},{2,6},{6,2},{3,7},{7,3},{8,12},{12,8},{9,1... | collective-permute-start | bytes 10760 | tf_op jit(solution)/shard_map/ppermute | solution.py:373
  35.0 0.7 copy-start.2

commit v7 on v6

--- a/solution.py
+++ b/solution.py
@@ -368,10 +368,11 @@
     place = lax.axis_index("inner").reshape(1)
     columns = [jnp.pad(table.T, ((0, 0), (0, slots - table.shape[0]))) for table in (a_cols, p_cols, gp_cols)]
     swap = ((0, 1), (1, 0))
-    a_other = lax.ppermute(a_vals, "inner", swap)
     table, table_sent = index(a_cols.shape[1], comp, place, jnp.concatenate(columns, axis=0))
     table_other = lax.ppermute(table_sent, "inner", swap)
-    p_other = lax.ppermute(p_vals, "inner", swap)
+    p_sent, a_sent, table = lax.optimization_barrier((p_vals, a_vals, table))
+    a_other = lax.ppermute(a_sent, "inner", swap)
+    p_other = lax.ppermute(p_sent, "inner", swap)
     spread, local = layout(place, table, p_vals)
     mixed = regroup(a_vals)
     mixed_other = regroup(a_other)

time: 102 us -> 102 us (level)
  Pallas kernels: 22.5 us -> 21.3 us
  waiting for transfers between devices: 28.6 us -> 29.8 us
    ppermute x1, waiting for transfers between devices: 4.92 us -> 6.16 us  [on_device(): table_other = lax.ppermute(table_sent, 'inner', swap)]
    pallas_call x2, Pallas kernels: 5.03 us -> 3.9 us  [regroup(): pl.pallas_call(regroup_kernel, out_shape=pltpu.HBM((rows, size, width), a...]
  transfers between devices with their start and end apart: 4 -> 4, of which waited for: 3 -> 3; matrix products, arithmetic and copies ran while one was open for 1% -> 1% of each run, Pallas kernels for 11% -> 10%
where the time goes in v7:
time: 102 us; the launch traced here: 101 us
  waiting for transfers between devices  29.8 us (29%)
  starting transfers between devices  25.1 us (25%)
  blocking collectives  22.9 us (22%)
  Pallas kernels  21.3 us (21%)
    all_to_all x1, blocking collectives, on_device(): lax.all_to_all(partial, ('outer', 'inner'), split_axis=0, concat_axis=0,...  22.9 us
    ppermute x1, waiting for transfers between devices, on_device(): a_other = lax.ppermute(a_sent, 'inner', swap)  22.6 us
    all_to_all x1, starting transfers between devices, on_device(): lax.all_to_all(outgoing, ('fine', 'inner', 'comp'), split_axis=0, concat_...  15.8 us
    pallas_call x1, Pallas kernels, product(): pl.pallas_call(product_kernel, out_shape=jax.ShapeDtypeStruct((NC * size,...  7.47 us
    ppermute x1, waiting for transfers between devices, on_device(): table_other = lax.ppermute(table_sent, 'inner', swap)  6.16 us
    pallas_call x1, Pallas kernels, index(): pl.pallas_call(lambda *refs: index_kernel(links, comp, *refs), out_shape=...  4.27 us
    pallas_call x2, Pallas kernels, regroup(): pl.pallas_call(regroup_kernel, out_shape=pltpu.HBM((rows, size, width), a...  3.9 us
    ppermute x1, starting transfers between devices, on_device(): table_other = lax.ppermute(table_sent, 'inner', swap)  3.55 us
  transfers between devices with their start and end apart: 4, of which 3 were waited for; matrix products, arithmetic and copies ran while one was open for 1% of the time, Pallas kernels for 10%

profile of v7, /device:TPU:6, one launch (start us, length us, event | category | flops | bytes accessed | tf_op | source)
XLA Modules:
  0.0 100.6 jit_solution(10406204127829141177)
XLA Ops:
  0.0 2.8 %pack.1 = bf16[16,2,4,64,128]{4,3,2,1,0:T(8,128)(2,1)} custom-call(s32[64]{0:T(128)} %send_hbm.1, bf16[12,64,256]{2,1,0:T(8,128)(2,1)} %p_hbm.1), custom_call_target="tpu_custom_call" | custom-call | tf_op jit(solution)/shard_map/pack/pallas_call | solution.py:65
  2.8 0.0 copy-start.4
  2.8 0.0 copy-start.5
  2.9 0.0 copy-start.6
  2.9 0.0 copy-start.1
  2.9 0.0 copy-start
  2.9 15.8 %all-to-all-start = ((bf16[128,64,128]{2,1,0:T(8,128)(2,1)}), bf16[128,64,128]{2,1,0:T(8,128)(2,1)S(1)}, u32[]{:S(2)}, u32[]{:S(2)}) async-start(bf16[128,64,128]{2,1,0:T(8,128)(2,1)} %bitcast.8), calls=%async_computation | async-start | bytes 4194304 | tf_op jit(solution)/shard_map/all_to_all | solution.py:367
  18.7 0.6 fusion.refs_1_
  19.3 4.3 %index.1 = (s32[7,128]{1,0:T(8,128)}, s32[7,128]{1,0:T(8,128)}) custom-call(s32[1]{0:T(128)} %bitcast.refs_0_.half_ref, s32[15,64]{1,0:T(8,128)} %fusion.refs_1_), custom_call_target="tpu_custom_call" | custom-call | tf_op jit(solution)/shard_map/index/pallas_call | solution.py:112
  23.6 3.4 %collective-permute-start = (bf16[12,64,448]{2,1,0:T(8,128)(2,1)S(1)}, bf16[12,64,448]{2,1,0:T(8,128)(2,1)S(1)}, u32[]{:S(2)}, u32[]{:S(2)}) collective-permute-start(bf16[12,64,448]{2,1,0:T(8,128)(2,1)S(1)} %copy-done.1), channel_id=1, source_target_pairs={{0,4},{4,0},{1,5},{5,1},{2,6},{6,2},{3,7},{7,3},{8,12},{12,8},{9,1... | collective-permute-start | bytes 2064392 | tf_op jit(solution)/shard_map/ppermute | solution.py:374
  27.0 2.5 %collective-permute-start.2 = (bf16[12,64,256]{2,1,0:T(8,128)(2,1)S(1)}, bf16[12,64,256]{2,1,0:T(8,128)(2,1)}, u32[]{:S(2)}, u32[]{:S(2)}) collective-permute-start(bf16[12,64,256]{2,1,0:T(8,128)(2,1)S(1)} %copy-done), channel_id=1, source_target_pairs={{0,4},{4,0},{1,5},{5,1},{2,6},{6,2},{3,7},{7,3},{8,12},{12,8},{9,1... | collective-permute-start | bytes 1179656 | tf_op jit(solution)/shard_map/ppermute | solution.py:375
  29.5 3.6 %collective-permute-start.1 = (s32[7,128]{1,0:T(8,128)}, s32[7,128]{1,0:T(8,128)S(1)}, u32[]{:S(2)}, u32[]{:S(2)}) collective-permute-start(s32[7,128]{1,0:T(8,128)} %get-tuple-element.18), channel_id=1, source_target_pairs={{0,4},{4,0},{1,5},{5,1},{2,6},{6,2},{3,7},{7,3},{8,12},{12,8},{9,1... | collective-permute-start | bytes 10760 | tf_op jit(solution)/shard_map/ppermute | solution.py:372
  33.0 2.0 %regroup.3.refs_6_ = bf16[12,64,448]{2,1,0:T(8,128)(2,1)} custom-call(bf16[12,64,448]{2,1,0:T(8,128)(2,1)S(1)} %copy-done.1), custom_call_target="tpu_custom_call" | custom-call | tf_op jit(solution)/shard_map/regroup/pallas_call | solution.py:189
  35.0 0.7 copy-done.2
  35.7 2.0 %layout.1 = (bf16[512,768]{1,0:T(8,128)(2,1)}, bf16[12,64,128]{2,1,0:T(8,128)(2,1)}) custom-call(s32[1]{0:T(128)} %bitcast.refs_0_.half_ref, s32[7,128]{1,0:T(8,128)S(1)} %copy-done.2, bf16[12,64,256]{2,1,0:T(8,128)(2,1)S(1)} %copy-done), custom_call_target="tpu_custom_call" | custom-call | tf_op jit(solution)/shard_map/layout/pallas_call | solution.py:155
  37.6 22.6 %collective-permute-done.a_ref = bf16[12,64,448]{2,1,0:T(8,128)(2,1)S(1)} collective-permute-done((bf16[12,64,448]{2,1,0:T(8,128)(2,1)S(1)}, bf16[12,64,448]{2,1,0:T(8,128)(2,1)S(1)}, u32[]{:S(2)}, u32[]{:S(2)}) %collective-permute-start) | collective-permute-done | bytes 688160 | tf_op jit(solution)/shard_map/ppermute | solution.py:374
  60.2 1.9 %regroup.2.refs_7_ = bf16[12,64,448]{2,1,0:T(8,128)(2,1)} custom-call(bf16[12,64,448]{2,1,0:T(8,128)(2,1)S(1)} %collective-permute-done.a_ref), custom_call_target="tpu_custom_call" | custom-call | tf_op jit(solution)/shard_map/regroup/pallas_call | solution.py:189
  62.2 6.2 %collective-permute-done.1.refs_2_ = s32[7,128]{1,0:T(8,128)S(1)} collective-permute-done((s32[7,128]{1,0:T(8,128)}, s32[7,128]{1,0:T(8,128)S(1)}, u32[]{:S(2)}, u32[]{:S(2)}) %collective-permute-start.1) | collective-permute-done | bytes 3616 | tf_op jit(solution)/shard_map/ppermute | solution.py:372
  68.4 0.0 collective-permute-done.2.refs_3_
  68.4 1.0 all-to-all-done.refs_8_
  69.3 0.0 copy-done.3
  69.3 7.5 %product.1 = bf16[512,512]{1,0:T(8,128)(2,1)S(1)} custom-call(s32[1]{0:T(128)} %bitcast.refs_0_.half_ref, s32[7,128]{1,0:T(8,128)S(1)} %copy-done.3, s32[7,128]{1,0:T(8,128)S(1)} %collective-permute-done.1.refs_2_, bf16[12,64,256]{2,1,0:T(8,128)(2,1)} %collective-permute-done.2.refs_3_, bf16[512,768]{1,0:T(8,128)(2,1)} %get-tuple-element.22.refs_4_, ...), custom_call_target="tpu_custom_call" | custom-call | tf_op jit(solution)/shard_map/product/pallas_call | solution.py:308
  76.8 22.9 %all_to_all.14.part_ref = bf16[8,64,512]{2,1,0:T(8,128)(2,1)S(1)} all-to-all(bf16[8,64,512]{2,1,0:T(8,128)(2,1)S(1)} %bitcast.7), channel_id=1, replica_groups=mesh['fine'=16,'outer'=4,'inner'=2,'comp'=4] {'outer','inner'}, dimensions={0} | all-to-all | bytes 1048576 | tf_op jit(solution)/shard_map/all_to_all | solution.py:381
  99.7 0.9 total.1
  (7 shorter events, 0.0 us)
Async XLA Ops:
  2.8 15.8 %copy-start.4 = (s32[12,7]{0,1:T(8,128)S(1)}, s32[12,7]{0,1:T(8,128)}, u32[]{:S(2)}) copy-start(s32[12,7]{0,1:T(8,128)} %param.7) | copy-start | bytes 1012
  2.8 15.8 %copy-start.5 = (s32[12,4]{0,1:T(4,128)S(1)}, s32[12,4]{0,1:T(4,128)}, u32[]{:S(2)}) copy-start(s32[12,4]{0,1:T(4,128)} %param.9) | copy-start | bytes 580
  2.9 15.8 %copy-start.6 = (s32[64,4]{0,1:T(4,128)S(1)}, s32[64,4]{0,1:T(4,128)}, u32[]{:S(2)}) copy-start(s32[64,4]{0,1:T(4,128)} %param.10) | copy-start | bytes 3076
  2.9 20.7 %copy-start.1 = (bf16[12,64,448]{2,1,0:T(8,128)(2,1)S(1)}, bf16[12,64,448]{2,1,0:T(8,128)(2,1)}, u32[]{:S(2)}) copy-start(bf16[12,64,448]{2,1,0:T(8,128)(2,1)} %a_ref.1) | copy-start | bytes 2064388
  2.9 24.1 %copy-start = (bf16[12,64,256]{2,1,0:T(8,128)(2,1)S(1)}, bf16[12,64,256]{2,1,0:T(8,128)(2,1)}, u32[]{:S(2)}) copy-start(bf16[12,64,256]{2,1,0:T(8,128)(2,1)} %p_hbm.1) | copy-start | bytes 1179652
  2.9 66.4 %all-to-all-start = ((bf16[128,64,128]{2,1,0:T(8,128)(2,1)}), bf16[128,64,128]{2,1,0:T(8,128)(2,1)S(1)}, u32[]{:S(2)}, u32[]{:S(2)}) async-start(bf16[128,64,128]{2,1,0:T(8,128)(2,1)} %bitcast.8), calls=%async_computation | async-start | bytes 4194304 | tf_op jit(solution)/shard_map/all_to_all | solution.py:367
  23.6 45.8 %copy-start.3 = (s32[7,128]{1,0:T(8,128)S(1)}, s32[7,128]{1,0:T(8,128)}, u32[]{:S(2)}) copy-start(s32[7,128]{1,0:T(8,128)} %get-tuple-element.16.table_ref.refs_1_) | copy-start | bytes 10756
  23.6 36.7 %collective-permute-start = (bf16[12,64,448]{2,1,0:T(8,128)(2,1)S(1)}, bf16[12,64,448]{2,1,0:T(8,128)(2,1)S(1)}, u32[]{:S(2)}, u32[]{:S(2)}) collective-permute-start(bf16[12,64,448]{2,1,0:T(8,128)(2,1)S(1)} %copy-done.1), channel_id=1, source_target_pairs={{0,4},{4,0},{1,5},{5,1},{2,6},{6,2},{3,7},{7,3},{8,12},{12,8},{9,1... | collective-permute-start | bytes 2064392 | tf_op jit(solution)/shard_map/ppermute | solution.py:374
  27.0 41.4 %collective-permute-start.2 = (bf16[12,64,256]{2,1,0:T(8,128)(2,1)S(1)}, bf16[12,64,256]{2,1,0:T(8,128)(2,1)}, u32[]{:S(2)}, u32[]{:S(2)}) collective-permute-start(bf16[12,64,256]{2,1,0:T(8,128)(2,1)S(1)} %copy-done), channel_id=1, source_target_pairs={{0,4},{4,0},{1,5},{5,1},{2,6},{6,2},{3,7},{7,3},{8,12},{12,8},{9,1... | collective-permute-start | bytes 1179656 | tf_op jit(solution)/shard_map/ppermute | solution.py:375
  29.5 38.9 %collective-permute-start.1 = (s32[7,128]{1,0:T(8,128)}, s32[7,128]{1,0:T(8,128)S(1)}, u32[]{:S(2)}, u32[]{:S(2)}) collective-permute-start(s32[7,128]{1,0:T(8,128)} %get-tuple-element.18), channel_id=1, source_target_pairs={{0,4},{4,0},{1,5},{5,1},{2,6},{6,2},{3,7},{7,3},{8,12},{12,8},{9,1... | collective-permute-start | bytes 10760 | tf_op jit(solution)/shard_map/ppermute | solution.py:372
  35.0 0.7 copy-start.2
